TPU v7x, 256 devices: a whole 4x4x8 slice. The times are simulated.
256 devices in a mesh: dp: 32 (over y_lo, z, core), seq: 8 (over y_hi, x).
Axes of the slice: x: 4, y: 4 (y_hi: 2, y_lo: 2; y = y_hi * 2 + y_lo), z: 8, core: 2. Of those that a mesh axis runs over, the one named last changes fastest.
Arguments:
- acts: bfloat16 [32768, 4096], P(('dp', 'seq')), may hold values from -24 to 24
- grad_out: bfloat16 [32768, 4096], P('dp', 'seq'), may hold values from -6 to 6
- proj_weight: bfloat16 [4096, 4096], P('dp', 'seq'), may hold values from -0.09375 to 0.09375
Outputs:
- grad_acts: float32 [32768, 4096], P(('dp', 'seq'))
- grad_weight: float32 [4096, 4096], P('dp', 'seq')
All inputs are finite; a program needn't handle non-finite values.
Results may differ from a plain program's by a relative error of at most 0.014.
Values may be sent and summed in bfloat16 or wider, within the bound.
No kernel may reach another device: no remote copies, remote signals or barrier semaphores. Data moves between devices by JAX's collectives and lax.ppermute only.
A program may use at most 64 MiB of HBM per device.

v0:
```python
import jax
import jax.numpy as jnp
from jax import lax
from jax.sharding import PartitionSpec as P


def rounded(value):
    return lax.optimization_barrier(value.astype(jnp.bfloat16)).astype(jnp.float32)


def per_device(acts, grad_out, proj_weight):
    tok_rows = acts.shape[0]
    total_tokens = tok_rows * lax.axis_size("seq") * lax.axis_size("dp")
    full_weight = lax.all_gather(proj_weight, "dp", axis=0, tiled=True)
    whole_term = lax.dot_general(
        grad_out, full_weight, (((1,), (1,)), ((), ())), preferred_element_type=jnp.float32
    )
    summed = lax.psum_scatter(
        whole_term.astype(jnp.bfloat16), "seq", scatter_dimension=0, tiled=True
    ).astype(jnp.float32)
    gathered = lax.all_gather(acts, "seq", axis=0, tiled=True)
    local_term = None
    local_term = rounded(
        lax.dot_general(
            gathered, grad_out, (((0,), (0,)), ((), ())), preferred_element_type=jnp.float32
        )
    )
    wsummed = lax.psum_scatter(local_term, "dp", scatter_dimension=0, tiled=True)
    grad_weight = wsummed / jnp.sqrt(jnp.float32(total_tokens))
    return (summed, grad_weight)


def solution(mesh):
    in_specs = (P(("dp", "seq"), None), P("dp", "seq"), P("dp", "seq"))
    out_specs = (P(("dp", "seq"), None), P("dp", "seq"))
    return jax.shard_map(
        per_device, mesh=mesh, in_specs=in_specs, out_specs=out_specs, check_vma=False
    )
```

profile of v0, /device:TPU:1, one launch (start us, length us, event | category | flops | bytes accessed | tf_op | source)
XLA Modules:
  0.0 452.2 jit_solution(2296822489435364021)
XLA Ops:
  7.2 0.0 copy-start
  7.2 0.0 all-gather.3.cloned.1.call-start
  7.2 0.7 all-gather.3.cloned.1.call-update
  7.9 0.0 all-gather.5.cloned.1.call-start
  8.0 0.7 all-gather.5.cloned.1.call-update
  8.7 0.0 reduce-scatter.3.cloned.1.call-start
  8.7 72.2 %all-gather.3.cloned.1.call-done = bf16[4096,512]{1,0:T(8,128)(2,1)} async-done(((bf16[128,512]{1,0:T(8,128)(2,1)}), bf16[4096,512]{1,0:T(8,128)(2,1)}) %all-gather.3.cloned.1.call-update) | async-done | bytes 4194320 | tf_op jit(solution)/shard_map/all_gather | solution.py:14
  80.9 0.0 copy-done
  80.9 8.9 %convolution_convert_fusion = bf16[1024,4096]{1,0:T(8,128)(2,1)} fusion(bf16[1024,512]{1,0:T(8,128)(2,1)S(1)} %copy-done, bf16[4096,512]{1,0:T(8,128)(2,1)} %all-gather.3.cloned.1.call-done), kind=kOutput, calls=%fused_computation | convolution fusion | flops 4299161600 | bytes 13631488 | tf_op jit(solution)/shard_map/dot_general | solution.py:15
  89.9 0.0 reduce-scatter.3.cloned.1.call-update
  89.9 0.0 reduce-scatter.5.cloned.1.call-start
  90.0 106.5 %all-gather.5.cloned.1.call-done = bf16[1024,4096]{1,0:T(8,128)(2,1)} async-done(((bf16[128,4096]{1,0:T(8,128)(2,1)}), bf16[1024,4096]{1,0:T(8,128)(2,1)}) %all-gather.5.cloned.1.call-update) | async-done | bytes 8388624 | tf_op jit(solution)/shard_map/all_gather | solution.py:21
  196.4 8.4 %convolution_convert_fusion.1 = bf16[4096,512]{1,0:T(8,128)(2,1)S(1)} fusion(bf16[1024,4096]{1,0:T(8,128)(2,1)} %all-gather.5.cloned.1.call-done, bf16[1024,512]{1,0:T(8,128)(2,1)S(1)} %copy-done), kind=kOutput, calls=%fused_computation.1 | convolution fusion | flops 4297064448 | bytes 13631488 | tf_op jit(solution)/shard_map/dot_general | solution.py:24
  204.8 4.4 convert_element_type.15
  209.2 0.0 reduce-scatter.5.cloned.1.call-update
  209.3 108.7 %reduce-scatter.3.cloned.1.call-done = bf16[128,4096]{1,0:T(8,128)(2,1)} async-done(((bf16[1024,4096]{1,0:T(8,128)(2,1)}), bf16[128,4096]{1,0:T(8,128)(2,1)}) %reduce-scatter.3.cloned.1.call-update) | async-done | bytes 1048592 | tf_op jit(solution)/shard_map/reduce_scatter | solution.py:18
  318.0 2.8 convert_element_type.13
  320.7 123.2 %reduce-scatter.5.cloned.1.call-done = f32[128,512]{1,0:T(8,128)} async-done(((f32[4096,512]{1,0:T(8,128)}), f32[128,512]{1,0:T(8,128)}) %reduce-scatter.5.cloned.1.call-update) | async-done | bytes 262160 | tf_op jit(solution)/shard_map/reduce_scatter | solution.py:28
  443.9 1.7 broadcast_multiply_fusion
Async XLA Ops:
  7.2 73.8 %copy-start = (bf16[1024,512]{1,0:T(8,128)(2,1)S(1)}, bf16[1024,512]{1,0:T(8,128)(2,1)}, u32[]{:S(2)}) copy-start(bf16[1024,512]{1,0:T(8,128)(2,1)} %param.4) | copy-start | bytes 3145732
  7.2 73.8 %all-gather.3.cloned.1.call-start = ((), (), s32[]{:S(2)}) async-start(), calls=%async_computation.2 | async-start | bytes 4325376 | tf_op jit(solution)/shard_map/all_gather | solution.py:14
  7.9 188.5 %all-gather.5.cloned.1.call-start = ((), (), s32[]{:S(2)}) async-start(), calls=%async_computation.4 | async-start | bytes 9437184 | tf_op jit(solution)/shard_map/all_gather | solution.py:21
  8.7 309.3 %reduce-scatter.3.cloned.1.call-start = ((), (), s32[]{:S(2)}) async-start(), calls=%async_computation.3 | async-start | bytes 9437184 | tf_op jit(solution)/shard_map/reduce_scatter | solution.py:18
  89.9 354.0 %reduce-scatter.5.cloned.1.call-start = ((), (), s32[]{:S(2)}) async-start(), calls=%async_computation.5 | async-start | bytes 8650752 | tf_op jit(solution)/shard_map/reduce_scatter | solution.py:28
Sparse Core Ops, SparseCore 0:
  9.9 71.0 all-gather.2
  83.6 112.8 all-gather.4
  200.6 117.3 reduce-scatter.2
  320.4 123.5 reduce-scatter.4
where the time goes:
time: 456 us; the launch traced here: 452 us
  waiting for transfers between devices  412 us (90%)
  matrix products  17.3 us (4%)
  between operations  13.8 us (3%)
  other arithmetic  8.86 us (2%)
    reduce_scatter x1, waiting for transfers between devices, per_device(): lax.psum_scatter(local_term, 'dp', scatter_dimension=0, tiled=True)  123 us
    reduce_scatter x1, waiting for transfers between devices, per_device(): lax.psum_scatter(whole_term.astype(jnp.bfloat16), 'seq', scatter_dimensio...  109 us
    all_gather x1, waiting for transfers between devices, per_device(): gathered = lax.all_gather(acts, 'seq', axis=0, tiled=True)  106 us
    all_gather x1, waiting for transfers between devices, per_device(): full_weight = lax.all_gather(proj_weight, 'dp', axis=0, tiled=True)  72.2 us
  transfers between devices with their start and end apart: 4, of which 4 were waited for; matrix products, arithmetic and copies ran while one was open for 5% of the time, Pallas kernels for 0%

commit v1 on v0

v1 whole, which is shorter than its diff:
```python
import jax
import jax.numpy as jnp
from jax import lax
from jax.sharding import Mesh, PartitionSpec as P

AXES = ("ylo", "z", "core", "yhi", "x")
SIZES = (2, 8, 2, 2, 4)
F32 = jnp.float32
BF16 = jnp.bfloat16


def from_x(value, offset):
    return lax.ppermute(value, "x", [((i + offset) % 4, i) for i in range(4)])


def swap(value, axis):
    return lax.ppermute(value, axis, [(0, 1), (1, 0)])


def rank16(ylo, core, x):
    return (ylo * 2 + core) * 4 + x


TO_BLOCK = [
    (rank16(x % 2, x // 2, (x + 2 * ylo + core) % 4), rank16(ylo, core, x))
    for ylo in range(2)
    for core in range(2)
    for x in range(4)
]
TO_OWNER = [(dst, src) for src, dst in TO_BLOCK]


def dot(a, b, contract):
    return lax.dot_general(a, b, ((contract[:1], contract[1:]), ((), ())), preferred_element_type=F32)


def per_device(acts, grad_out, weight):
    ylo, core = lax.axis_index("ylo"), lax.axis_index("core")
    yhi, x = lax.axis_index("yhi"), lax.axis_index("x")

    w = lax.ppermute(weight, ("ylo", "core", "x"), TO_BLOCK)
    w_other = swap(w, "ylo")
    w = jnp.concatenate([jnp.where(ylo == 0, w, w_other), jnp.where(ylo == 0, w_other, w)], axis=1)
    w = lax.all_gather(w, "z", axis=0, tiled=True)
    w_other = swap(w, "core")
    w_even = jnp.where(core == 0, w, w_other)
    w_odd = jnp.where(core == 0, w_other, w)

    blocks = acts.reshape(128, 2, 8, 2, 128).transpose(3, 1, 0, 2, 4).reshape(4, 128, 1024)

    def block_of(stack, k):
        return lax.dynamic_index_in_dim(stack, (x + k) % 4, 0, keepdims=False)

    half = jnp.zeros((4, 128, 1024), BF16)
    for k in range(4):
        piece = block_of(blocks, -k)
        piece = from_x(piece, k) if k else piece
        half = lax.dynamic_update_index_in_dim(half, piece, (x + k) % 4, 0)
    other = swap(half, "yhi")
    tokens = jnp.stack([jnp.where(yhi == 0, half, other), jnp.where(yhi == 0, other, half)])
    tokens = tokens.reshape(1024, 1024)

    g0 = grad_out
    g1 = from_x(g0, 1)
    g3 = from_x(g0, -1)
    g2 = jnp.concatenate([from_x(g1[:512], 1), from_x(g3[512:], -1)], axis=0)
    g = [g0, g1, g2, g3]

    terms = [dot(tokens, g_k, (0, 0)).astype(BF16) for g_k in g]
    keep = [jnp.where(core == 0, terms[0], terms[1]), jnp.where(core == 0, terms[2], terms[3])]
    give = [jnp.where(core == 0, terms[1], terms[0]), jnp.where(core == 0, terms[3], terms[2])]
    s = [(a.astype(F32) + swap(b, "core").astype(F32)).astype(BF16) for a, b in zip(keep, give)]
    keep = jnp.where(ylo == 0, s[0], s[1])
    give = jnp.where(ylo == 0, s[1], s[0])
    s = (keep.astype(F32) + swap(give, "ylo").astype(F32)).astype(BF16)
    s = lax.psum_scatter(s, "z", scatter_dimension=0, tiled=True)
    s = lax.ppermute(s, ("ylo", "core", "x"), TO_OWNER)
    grad_weight = s.astype(F32) / jnp.sqrt(F32(32768))

    part = dot(jnp.concatenate([g0, g2], axis=1), w_even, (1, 1))
    part = part + dot(jnp.concatenate([g1, g3], axis=1), w_odd, (1, 1))
    part = part.reshape(2, 512, 1024)
    give = lax.dynamic_index_in_dim(part, 1 - yhi, 0, keepdims=False).astype(BF16)
    mine = lax.dynamic_index_in_dim(part, yhi, 0, keepdims=False)
    mine = mine + swap(give, "yhi").astype(F32)
    mine = mine.reshape(4, 128, 1024)
    out = jnp.zeros((4, 128, 1024), F32)
    for k in range(4):
        piece = block_of(mine, -k)
        piece = from_x(piece.astype(BF16), k).astype(F32) if k else piece
        out = lax.dynamic_update_index_in_dim(out, piece, (x + k) % 4, 0)
    out = out.reshape(2, 2, 128, 8, 128).transpose(2, 1, 3, 0, 4).reshape(128, 4096)
    return (out, grad_weight)


def solution(mesh):
    fine = Mesh(mesh.devices.reshape(SIZES), AXES)
    rows = P(AXES, None)
    blocks = P(("ylo", "z", "core"), ("yhi", "x"))
    return jax.shard_map(
        per_device,
        mesh=fine,
        in_specs=(rows, blocks, blocks),
        out_specs=(rows, blocks),
        check_vma=False,
    )
```

time: 456 us -> 233 us (0.51)
  waiting for transfers between devices: 412 us -> 119 us
  starting transfers between devices: 0.16 us -> 46.2 us
  local copies, waits for them, and re-layouts: 0.01 us -> 20.7 us
  other arithmetic: 8.86 us -> 13.8 us
    reduce_scatter x2 -> x1, waiting for transfers between devices: 232 us -> 19.4 us  [per_device(): s = lax.psum_scatter(s, 'z', scatter_dimension=0, tiled=True)]
    all_gather x2 -> x1, waiting for transfers between devices: 179 us -> 16.6 us  [per_device(): w = lax.all_gather(w, 'z', axis=0, tiled=True)]
    ppermute x0 -> x19, waiting for transfers between devices: none -> 83.2 us  [the longest x7 46.1 us: swap(): return lax.ppermute(value, axis, [(0, 1), (1, 0)])]
    ppermute x0 -> x19, starting transfers between devices: none -> 46.1 us  [the longest x7 21.3 us: swap(): return lax.ppermute(value, axis, [(0, 1), (1, 0)])]
    unnamed x2 -> x27, local copies, waits for them, and re-layouts: 0.01 us -> 9.8 us
    convert_element_type x2 -> x1, other arithmetic: 7.18 us -> 1.39 us  [per_device(): s = (keep.astype(F32) + swap(give, 'ylo').astype(F32)).astype(BF16)]
    broadcast_in_dim x0 -> x3, other arithmetic: none -> 4.57 us  [per_device(): out = lax.dynamic_update_index_in_dim(out, piece, (x + k) % 4, 0)]
    dot_general x2 -> x6, matrix products: 17.3 us -> 18.2 us  [dot(): lax.dot_general(a, b, ((contract[:1], contract[1:]), ((), ())), preferred...]
  transfers between devices with their start and end apart: 4 -> 21, of which waited for: 4 -> 11; matrix products, arithmetic and copies ran while one was open for 5% -> 16% of each run, Pallas kernels for 0% -> 0%
where the time goes in v1:
time: 233 us
  waiting for transfers between devices  119 us (51%)
  starting transfers between devices  46.2 us (20%)
  local copies, waits for them, and re-layouts  20.7 us (9%)
  matrix products  18.2 us (8%)
  between operations  14.6 us (6%)
  other arithmetic  13.8 us (6%)
    ppermute x7, waiting for transfers between devices, swap(): return lax.ppermute(value, axis, [(0, 1), (1, 0)])  46.1 us
    ppermute x10, waiting for transfers between devices, from_x(): return lax.ppermute(value, 'x', [((i + offset) % 4, i) for i in range(4)])  34.6 us
    ppermute x7, starting transfers between devices, swap(): return lax.ppermute(value, axis, [(0, 1), (1, 0)])  21.3 us
    reduce_scatter x1, waiting for transfers between devices, per_device(): s = lax.psum_scatter(s, 'z', scatter_dimension=0, tiled=True)  19.4 us
    dot_general x6, matrix products, dot(): lax.dot_general(a, b, ((contract[:1], contract[1:]), ((), ())), preferred...  18.2 us
    all_gather x1, waiting for transfers between devices, per_device(): w = lax.all_gather(w, 'z', axis=0, tiled=True)  16.6 us
    ppermute x10, starting transfers between devices, from_x(): return lax.ppermute(value, 'x', [((i + offset) % 4, i) for i in range(4)])  9.94 us
    unnamed x27, local copies, waits for them, and re-layouts  9.8 us
  transfers between devices with their start and end apart: 21, of which 11 were waited for; matrix products, arithmetic and copies ran while one was open for 16% of the time, Pallas kernels for 0%

profile of v1, /device:TPU:1, one launch (start us, length us, event | category | flops | bytes accessed | tf_op | source)
XLA Modules:
  0.0 232.7 jit_solution(10514562266721247765)
XLA Ops:
  10.0 3.3 %collective-permute-start.11 = (bf16[128,1024]{1,0:T(8,128)(2,1)}, bf16[128,1024]{1,0:T(8,128)(2,1)S(1)}, u32[]{:S(2)}, u32[]{:S(2)}) collective-permute-start(bf16[128,1024]{1,0:T(8,128)(2,1)} %bitcast.16), channel_id=1, source_target_pairs={{1,0},{2,1},{3,2},{0,3},{5,4},{6,5},{7,6},{4,7},{9,8},{10,9},{11,1... | collective-permute-start | bytes 786440 | tf_op jit(solution)/shard_map/ppermute | solution.py:13
  19.2 7.3 %collective-permute-start.4 = (bf16[128,512]{1,0:T(8,128)(2,1)}, bf16[128,512]{1,0:T(8,128)(2,1)S(1)}, u32[]{:S(2)}, u32[]{:S(2)}) collective-permute-start(bf16[128,512]{1,0:T(8,128)(2,1)} %param.5), channel_id=1, source_target_pairs={{0,0},{129,1},{10,2},{139,3},{1,8},{130,9},{11,10},{136,11},{2,128... | collective-permute-start | bytes 393224 | tf_op jit(solution)/shard_map/ppermute | solution.py:41
  26.5 16.3 %collective-permute-done.12 = bf16[128,1024]{1,0:T(8,128)(2,1)S(1)} collective-permute-done((bf16[128,1024]{1,0:T(8,128)(2,1)}, bf16[128,1024]{1,0:T(8,128)(2,1)S(1)}, u32[]{:S(2)}, u32[]{:S(2)}) %collective-permute-start.12) | collective-permute-done | bytes 262176 | tf_op jit(solution)/shard_map/ppermute | solution.py:13
  42.8 7.1 %collective-permute-done.13 = bf16[128,1024]{1,0:T(8,128)(2,1)S(1)} collective-permute-done((bf16[128,1024]{1,0:T(8,128)(2,1)}, bf16[128,1024]{1,0:T(8,128)(2,1)S(1)}, u32[]{:S(2)}, u32[]{:S(2)}) %collective-permute-start.13) | collective-permute-done | bytes 262176 | tf_op jit(solution)/shard_map/ppermute | solution.py:13
  49.9 3.0 %collective-permute-start.14 = (bf16[4,128,1024]{2,1,0:T(8,128)(2,1)S(1)}, bf16[4,128,1024]{2,1,0:T(8,128)(2,1)S(1)}, u32[]{:S(2)}, u32[]{:S(2)}) collective-permute-start(bf16[4,128,1024]{2,1,0:T(8,128)(2,1)S(1)} %bitcast_dynamic-update-slice_fusion), channel_id=1, source_target_pairs={{0,4},{4,0},{1,5},{5,1},{2,6},{6,2},{3,7},{7,3},{8,12},{12,8},{9,1... | collective-permute-start | bytes 3145736 | tf_op jit(solution)/shard_map/ppermute | solution.py:17
  55.4 21.8 %collective-permute-done.5 = bf16[128,512]{1,0:T(8,128)(2,1)S(1)} collective-permute-done((bf16[128,512]{1,0:T(8,128)(2,1)S(1)}, bf16[128,512]{1,0:T(8,128)(2,1)S(1)}, u32[]{:S(2)}, u32[]{:S(2)}) %collective-permute-start.5) | collective-permute-done | bytes 131104 | tf_op jit(solution)/shard_map/ppermute | solution.py:17
  83.5 2.6 %broadcast_select_fusion.1 = (bf16[1024,512]{1,0:T(8,128)(2,1)}, bf16[1024,512]{1,0:T(8,128)(2,1)}) fusion(bf16[1024,512]{1,0:T(8,128)(2,1)S(1)} %convolution_convert_fusion.3, pred[]{:T(512)S(6)} %eq.35, bf16[1024,1024]{1,0:T(8,128)(2,1)S(1)} %bitcast.60, bf16[1024,512]{1,0:T(8,128)(2,1)S(1)} %copy-done.6), kind=kOutput, calls=%fused_computation.27 | convolution fusion | flops 1074790400 | bytes 6291457 | tf_op jit(solution)/shard_map/dot_general | solution.py:34
  86.1 3.6 %collective-permute-start.15 = (bf16[1024,512]{1,0:T(8,128)(2,1)}, bf16[1024,512]{1,0:T(8,128)(2,1)S(1)}, u32[]{:S(2)}, u32[]{:S(2)}) collective-permute-start(bf16[1024,512]{1,0:T(8,128)(2,1)} %get-tuple-element.20), channel_id=1, source_target_pairs={{0,8},{8,0},{1,9},{9,1},{2,10},{10,2},{3,11},{11,3},{4,12},{12,4},... | collective-permute-start | bytes 3145736 | tf_op jit(solution)/shard_map/ppermute | solution.py:17
  92.4 4.2 %broadcast_select_fusion = (bf16[1024,512]{1,0:T(8,128)(2,1)}, bf16[1024,512]{1,0:T(8,128)(2,1)}) fusion(bf16[1024,512]{1,0:T(8,128)(2,1)S(1)} %convolution_convert_fusion.1, pred[]{:T(512)S(6)} %eq.35, bf16[1024,1024]{1,0:T(8,128)(2,1)S(1)} %bitcast.62, bf16[1024,512]{1,0:T(8,128)(2,1)} %collective-permute-done.2), kind=kOutput, calls=%fused_computation.26 | convolution fusion | flops 1074790400 | bytes 6291457 | tf_op jit(solution)/shard_map/dot_general | solution.py:34
  96.7 4.0 %collective-permute-start.16 = (bf16[1024,512]{1,0:T(8,128)(2,1)}, bf16[1024,512]{1,0:T(8,128)(2,1)S(1)}, u32[]{:S(2)}, u32[]{:S(2)}) collective-permute-start(bf16[1024,512]{1,0:T(8,128)(2,1)} %get-tuple-element.22), channel_id=1, source_target_pairs={{0,8},{8,0},{1,9},{9,1},{2,10},{10,2},{3,11},{11,3},{4,12},{12,4},... | collective-permute-start | bytes 3145736 | tf_op jit(solution)/shard_map/ppermute | solution.py:17
  100.7 16.6 %all-gather.2.cloned.1.call-done = bf16[1024,1024]{1,0:T(8,128)(2,1)} async-done(((bf16[128,1024]{1,0:T(8,128)(2,1)}), bf16[1024,1024]{1,0:T(8,128)(2,1)}) %all-gather.2.cloned.1.call-update) | async-done | bytes 2097168 | tf_op jit(solution)/shard_map/all_gather | solution.py:44
  117.3 4.6 %collective-permute-start.6 = (bf16[1024,1024]{1,0:T(8,128)(2,1)}, bf16[1024,1024]{1,0:T(8,128)(2,1)}, u32[]{:S(2)}, u32[]{:S(2)}) collective-permute-start(bf16[1024,1024]{1,0:T(8,128)(2,1)} %all-gather.2.cloned.1.call-done), channel_id=1, source_target_pairs={{0,8},{8,0},{1,9},{9,1},{2,10},{10,2},{3,11},{11,3},{4,12},{12,4},... | collective-permute-start | bytes 6291464 | tf_op jit(solution)/shard_map/ppermute | solution.py:17
  123.2 4.1 %broadcast_select_fusion.2 = (bf16[1024,512]{1,0:T(8,128)(2,1)}, bf16[1024,512]{1,0:T(8,128)(2,1)S(1)}, bf16[1024,512]{1,0:T(8,128)(2,1)S(1)}) fusion(pred[]{:T(512)S(6)} %eq.36, bf16[1024,512]{1,0:T(8,128)(2,1)} %copy-done.2, bf16[1024,512]{1,0:T(8,128)(2,1)S(1)} %convolution_convert_fusion.3, bf16[1024,512]{1,0:T(8,128)(2,1)} %get-tuple-element.21, ...), kind=kLoop, calls=%fused_computation.28 | loop fusion | flops 5767168 | bytes 9437186 | tf_op jit(solution)/shard_map/jit(_where)/select_n | solution.py:74
  128.3 24.3 %collective-permute-done.17 = bf16[1024,512]{1,0:T(8,128)(2,1)S(1)} collective-permute-done((bf16[1024,512]{1,0:T(8,128)(2,1)}, bf16[1024,512]{1,0:T(8,128)(2,1)S(1)}, u32[]{:S(2)}, u32[]{:S(2)}) %collective-permute-start.17) | collective-permute-done | bytes 1048608 | tf_op jit(solution)/shard_map/ppermute | solution.py:17
  154.0 4.8 %fusion.4 = f32[1024,1024]{1,0:T(8,128)S(1)} fusion(bf16[1024,512]{1,0:T(8,128)(2,1)} %collective-permute-done.2, bf16[1024,512]{1,0:T(8,128)(2,1)} %copy-done.5, bf16[1024,1024]{1,0:T(8,128)(2,1)} %collective-permute-done.6, bf16[1024,1024]{1,0:T(8,128)(2,1)} %all-gather.2.cloned.1.call-done, pred[]{:T(512)S(6)} %eq.35), kind=kOutput, calls=%fused_computation.4 | convolution fusion | flops 2152726528 | bytes 10485761 | tf_op jit(solution)/shard_map/dot_general | solution.py:34
  158.8 4.0 %fusion.12 = f32[1024,1024]{1,0:T(8,128)S(1)} fusion(f32[1024,1024]{1,0:T(8,128)S(1)} %fusion.4, bf16[1024,1024]{1,0:T(8,128)(2,1)S(1)} %copy-done.9, bf16[1024,1024]{1,0:T(8,128)(2,1)} %collective-permute-done.6, pred[]{:T(512)S(6)} %eq.35, bf16[1024,512]{1,0:T(8,128)(2,1)S(1)} %copy-done.8, bf16[1024,512]{1,0:T(8,128)(2,1)S(1)} %copy-done.11), kind=kOutput, calls=%fused_computation.18 | convolution fusion | flops 2153775104 | bytes 14680065 | tf_op jit(solution)/shard_map/dot_general | solution.py:34
  165.0 2.6 %collective-permute-start.7 = (bf16[512,1024]{1,0:T(8,128)(2,1)S(1)}, bf16[512,1024]{1,0:T(8,128)(2,1)S(1)}, u32[]{:S(2)}, u32[]{:S(2)}) collective-permute-start(bf16[512,1024]{1,0:T(8,128)(2,1)S(1)} %fusion.17), channel_id=1, source_target_pairs={{0,4},{4,0},{1,5},{5,1},{2,6},{6,2},{3,7},{7,3},{8,12},{12,8},{9,1... | collective-permute-start | bytes 3145736 | tf_op jit(solution)/shard_map/ppermute | solution.py:17
  167.5 19.4 %reduce-scatter.2.cloned.1.call-done = bf16[128,512]{1,0:T(8,128)(2,1)} async-done(((bf16[1024,512]{1,0:T(8,128)(2,1)}), bf16[128,512]{1,0:T(8,128)(2,1)}) %reduce-scatter.2.cloned.1.call-update) | async-done | bytes 131088 | tf_op jit(solution)/shard_map/reduce_scatter | solution.py:76
  187.0 7.6 %collective-permute-start.18 = (bf16[128,512]{1,0:T(8,128)(2,1)}, bf16[128,512]{1,0:T(8,128)(2,1)S(1)}, u32[]{:S(2)}, u32[]{:S(2)}) collective-permute-start(bf16[128,512]{1,0:T(8,128)(2,1)} %reduce-scatter.2.cloned.1.call-done), channel_id=1, source_target_pairs={{0,0},{1,129},{2,10},{3,139},{8,1},{9,130},{10,11},{11,136},{128,2... | collective-permute-start | bytes 393224 | tf_op jit(solution)/shard_map/ppermute | solution.py:77
  197.4 2.5 %collective-permute-done.18 = bf16[128,512]{1,0:T(8,128)(2,1)S(1)} collective-permute-done((bf16[128,512]{1,0:T(8,128)(2,1)}, bf16[128,512]{1,0:T(8,128)(2,1)S(1)}, u32[]{:S(2)}, u32[]{:S(2)}) %collective-permute-start.18) | collective-permute-done | bytes 131104 | tf_op jit(solution)/shard_map/ppermute | solution.py:77
  202.5 3.3 %collective-permute-done.8 = bf16[128,1024]{1,0:T(8,128)(2,1)} collective-permute-done((bf16[128,1024]{1,0:T(8,128)(2,1)S(1)}, bf16[128,1024]{1,0:T(8,128)(2,1)}, u32[]{:S(2)}, u32[]{:S(2)}) %collective-permute-start.8) | collective-permute-done | bytes 262176 | tf_op jit(solution)/shard_map/ppermute | solution.py:13
  207.0 3.0 %collective-permute-done.9 = bf16[128,1024]{1,0:T(8,128)(2,1)} collective-permute-done((bf16[128,1024]{1,0:T(8,128)(2,1)}, bf16[128,1024]{1,0:T(8,128)(2,1)}, u32[]{:S(2)}, u32[]{:S(2)}) %collective-permute-start.9) | collective-permute-done | bytes 262176 | tf_op jit(solution)/shard_map/ppermute | solution.py:13
  213.0 3.6 %collective-permute-done.10 = bf16[128,1024]{1,0:T(8,128)(2,1)} collective-permute-done((bf16[128,1024]{1,0:T(8,128)(2,1)S(1)}, bf16[128,1024]{1,0:T(8,128)(2,1)}, u32[]{:S(2)}, u32[]{:S(2)}) %collective-permute-start.10) | collective-permute-done | bytes 262176 | tf_op jit(solution)/shard_map/ppermute | solution.py:13
  223.0 2.9 %copy.25 = f32[128,4096]{1,0:T(8,128)} copy(f32[128,4096]{0,1:T(8,128)} %bitcast.52) | data formatting | bytes 4194304
  (91 shorter events, 41.6 us)
Async XLA Ops:
  7.2 110.1 %all-gather.2.cloned.1.call-start = ((), (), s32[]{:S(2)}) async-start(), calls=%async_computation.1 | async-start | bytes 2359296 | tf_op jit(solution)/shard_map/all_gather | solution.py:44
  10.0 9.2 %collective-permute-start.11 = (bf16[128,1024]{1,0:T(8,128)(2,1)}, bf16[128,1024]{1,0:T(8,128)(2,1)S(1)}, u32[]{:S(2)}, u32[]{:S(2)}) collective-permute-start(bf16[128,1024]{1,0:T(8,128)(2,1)} %bitcast.16), channel_id=1, source_target_pairs={{1,0},{2,1},{3,2},{0,3},{5,4},{6,5},{7,6},{4,7},{9,8},{10,9},{11,1... | collective-permute-start | bytes 786440 | tf_op jit(solution)/shard_map/ppermute | solution.py:13
  13.3 64.7 %collective-permute-start = (bf16[1024,512]{1,0:T(8,128)(2,1)}, bf16[1024,512]{1,0:T(8,128)(2,1)S(1)}, u32[]{:S(2)}, u32[]{:S(2)}) collective-permute-start(bf16[1024,512]{1,0:T(8,128)(2,1)} %param.4), channel_id=1, source_target_pairs={{1,0},{2,1},{3,2},{0,3},{5,4},{6,5},{7,6},{4,7},{9,8},{10,9},{11,1... | collective-permute-start | bytes 3145736 | tf_op jit(solution)/shard_map/ppermute | solution.py:13
  13.8 64.3 %collective-permute-start.2 = (bf16[1024,512]{1,0:T(8,128)(2,1)}, bf16[1024,512]{1,0:T(8,128)(2,1)}, u32[]{:S(2)}, u32[]{:S(2)}) collective-permute-start(bf16[1024,512]{1,0:T(8,128)(2,1)} %param.4), channel_id=1, source_target_pairs={{3,0},{0,1},{1,2},{2,3},{7,4},{4,5},{5,6},{6,7},{11,8},{8,9},{9,10... | collective-permute-start | bytes 3145736 | tf_op jit(solution)/shard_map/ppermute | solution.py:13
  15.6 27.2 %collective-permute-start.12 = (bf16[128,1024]{1,0:T(8,128)(2,1)}, bf16[128,1024]{1,0:T(8,128)(2,1)S(1)}, u32[]{:S(2)}, u32[]{:S(2)}) collective-permute-start(bf16[128,1024]{1,0:T(8,128)(2,1)} %bitcast.18), channel_id=1, source_target_pairs={{2,0},{3,1},{0,2},{1,3},{6,4},{7,5},{4,6},{5,7},{10,8},{11,9},{8,1... | collective-permute-start | bytes 786440 | tf_op jit(solution)/shard_map/ppermute | solution.py:13
  17.0 32.9 %collective-permute-start.13 = (bf16[128,1024]{1,0:T(8,128)(2,1)}, bf16[128,1024]{1,0:T(8,128)(2,1)S(1)}, u32[]{:S(2)}, u32[]{:S(2)}) collective-permute-start(bf16[128,1024]{1,0:T(8,128)(2,1)} %bitcast.20), channel_id=1, source_target_pairs={{3,0},{0,1},{1,2},{2,3},{7,4},{4,5},{5,6},{6,7},{11,8},{8,9},{9,10... | collective-permute-start | bytes 786440 | tf_op jit(solution)/shard_map/ppermute | solution.py:13
  19.2 33.8 %collective-permute-start.4 = (bf16[128,512]{1,0:T(8,128)(2,1)}, bf16[128,512]{1,0:T(8,128)(2,1)S(1)}, u32[]{:S(2)}, u32[]{:S(2)}) collective-permute-start(bf16[128,512]{1,0:T(8,128)(2,1)} %param.5), channel_id=1, source_target_pairs={{0,0},{129,1},{10,2},{139,3},{1,8},{130,9},{11,10},{136,11},{2,128... | collective-permute-start | bytes 393224 | tf_op jit(solution)/shard_map/ppermute | solution.py:41
  49.9 30.8 %collective-permute-start.14 = (bf16[4,128,1024]{2,1,0:T(8,128)(2,1)S(1)}, bf16[4,128,1024]{2,1,0:T(8,128)(2,1)S(1)}, u32[]{:S(2)}, u32[]{:S(2)}) collective-permute-start(bf16[4,128,1024]{2,1,0:T(8,128)(2,1)S(1)} %bitcast_dynamic-update-slice_fusion), channel_id=1, source_target_pairs={{0,4},{4,0},{1,5},{5,1},{2,6},{6,2},{3,7},{7,3},{8,12},{12,8},{9,1... | collective-permute-start | bytes 3145736 | tf_op jit(solution)/shard_map/ppermute | solution.py:17
  52.9 24.2 %collective-permute-start.5 = (bf16[128,512]{1,0:T(8,128)(2,1)S(1)}, bf16[128,512]{1,0:T(8,128)(2,1)S(1)}, u32[]{:S(2)}, u32[]{:S(2)}) collective-permute-start(bf16[128,512]{1,0:T(8,128)(2,1)S(1)} %collective-permute-done.4), channel_id=1, source_target_pairs={{0,128},{128,0},{1,129},{129,1},{2,130},{130,2},{3,131},{131,3},{4... | collective-permute-start | bytes 393224 | tf_op jit(solution)/shard_map/ppermute | solution.py:17
  77.9 109.0 %reduce-scatter.2.cloned.1.call-start = ((), (), s32[]{:S(2)}) async-start(), calls=%async_computation.2 | async-start | bytes 1179648 | tf_op jit(solution)/shard_map/reduce_scatter | solution.py:76
  78.1 11.7 %collective-permute-start.1 = (bf16[512,512]{1,0:T(8,128)(2,1)S(1)}, bf16[512,512]{1,0:T(8,128)(2,1)S(1)}, u32[]{:S(2)}, u32[]{:S(2)}) collective-permute-start(bf16[512,512]{1,0:T(8,128)(2,1)S(1)} %slice.8), channel_id=1, source_target_pairs={{1,0},{2,1},{3,2},{0,3},{5,4},{6,5},{7,6},{4,7},{9,8},{10,9},{11,1... | collective-permute-start | bytes 1572872 | tf_op jit(solution)/shard_map/ppermute | solution.py:13
  79.5 11.6 %collective-permute-start.3 = (bf16[512,512]{1,0:T(8,128)(2,1)S(1)}, bf16[512,512]{1,0:T(8,128)(2,1)S(1)}, u32[]{:S(2)}, u32[]{:S(2)}) collective-permute-start(bf16[512,512]{1,0:T(8,128)(2,1)S(1)} %slice.9), channel_id=1, source_target_pairs={{3,0},{0,1},{1,2},{2,3},{7,4},{4,5},{5,6},{6,7},{11,8},{8,9},{9,10... | collective-permute-start | bytes 1572872 | tf_op jit(solution)/shard_map/ppermute | solution.py:13
  86.1 35.8 %collective-permute-start.15 = (bf16[1024,512]{1,0:T(8,128)(2,1)}, bf16[1024,512]{1,0:T(8,128)(2,1)S(1)}, u32[]{:S(2)}, u32[]{:S(2)}) collective-permute-start(bf16[1024,512]{1,0:T(8,128)(2,1)} %get-tuple-element.20), channel_id=1, source_target_pairs={{0,8},{8,0},{1,9},{9,1},{2,10},{10,2},{3,11},{11,3},{4,12},{12,4},... | collective-permute-start | bytes 3145736 | tf_op jit(solution)/shard_map/ppermute | solution.py:17
  96.7 25.2 %collective-permute-start.16 = (bf16[1024,512]{1,0:T(8,128)(2,1)}, bf16[1024,512]{1,0:T(8,128)(2,1)S(1)}, u32[]{:S(2)}, u32[]{:S(2)}) collective-permute-start(bf16[1024,512]{1,0:T(8,128)(2,1)} %get-tuple-element.22), channel_id=1, source_target_pairs={{0,8},{8,0},{1,9},{9,1},{2,10},{10,2},{3,11},{11,3},{4,12},{12,4},... | collective-permute-start | bytes 3145736 | tf_op jit(solution)/shard_map/ppermute | solution.py:17
  117.3 36.7 %collective-permute-start.6 = (bf16[1024,1024]{1,0:T(8,128)(2,1)}, bf16[1024,1024]{1,0:T(8,128)(2,1)}, u32[]{:S(2)}, u32[]{:S(2)}) collective-permute-start(bf16[1024,1024]{1,0:T(8,128)(2,1)} %all-gather.2.cloned.1.call-done), channel_id=1, source_target_pairs={{0,8},{8,0},{1,9},{9,1},{2,10},{10,2},{3,11},{11,3},{4,12},{12,4},... | collective-permute-start | bytes 6291464 | tf_op jit(solution)/shard_map/ppermute | solution.py:17
  127.3 25.2 %collective-permute-start.17 = (bf16[1024,512]{1,0:T(8,128)(2,1)}, bf16[1024,512]{1,0:T(8,128)(2,1)S(1)}, u32[]{:S(2)}, u32[]{:S(2)}) collective-permute-start(bf16[1024,512]{1,0:T(8,128)(2,1)} %get-tuple-element.6), channel_id=1, source_target_pairs={{0,128},{128,0},{1,129},{129,1},{2,130},{130,2},{3,131},{131,3},{4... | collective-permute-start | bytes 3145736 | tf_op jit(solution)/shard_map/ppermute | solution.py:17
  154.0 4.8 %copy-start.8 = (bf16[1024,512]{1,0:T(8,128)(2,1)S(1)}, bf16[1024,512]{1,0:T(8,128)(2,1)}, u32[]{:S(2)}) copy-start(bf16[1024,512]{1,0:T(8,128)(2,1)} %copy-done.7) | copy-start | bytes 3145732
  154.0 4.8 %copy-start.9 = (bf16[1024,1024]{1,0:T(8,128)(2,1)S(1)}, bf16[1024,1024]{1,0:T(8,128)(2,1)}, u32[]{:S(2)}) copy-start(bf16[1024,1024]{1,0:T(8,128)(2,1)} %all-gather.2.cloned.1.call-done) | copy-start | bytes 6291460
  154.0 4.8 %copy-start.11 = (bf16[1024,512]{1,0:T(8,128)(2,1)S(1)}, bf16[1024,512]{1,0:T(8,128)(2,1)}, u32[]{:S(2)}) copy-start(bf16[1024,512]{1,0:T(8,128)(2,1)} %param.4) | copy-start | bytes 3145732
  165.0 29.7 %collective-permute-start.7 = (bf16[512,1024]{1,0:T(8,128)(2,1)S(1)}, bf16[512,1024]{1,0:T(8,128)(2,1)S(1)}, u32[]{:S(2)}, u32[]{:S(2)}) collective-permute-start(bf16[512,1024]{1,0:T(8,128)(2,1)S(1)} %fusion.17), channel_id=1, source_target_pairs={{0,4},{4,0},{1,5},{5,1},{2,6},{6,2},{3,7},{7,3},{8,12},{12,8},{9,1... | collective-permute-start | bytes 3145736 | tf_op jit(solution)/shard_map/ppermute | solution.py:17
  187.0 12.9 %collective-permute-start.18 = (bf16[128,512]{1,0:T(8,128)(2,1)}, bf16[128,512]{1,0:T(8,128)(2,1)S(1)}, u32[]{:S(2)}, u32[]{:S(2)}) collective-permute-start(bf16[128,512]{1,0:T(8,128)(2,1)} %reduce-scatter.2.cloned.1.call-done), channel_id=1, source_target_pairs={{0,0},{1,129},{2,10},{3,139},{8,1},{9,130},{10,11},{11,136},{128,2... | collective-permute-start | bytes 393224 | tf_op jit(solution)/shard_map/ppermute | solution.py:77
  197.4 8.4 %collective-permute-start.8 = (bf16[128,1024]{1,0:T(8,128)(2,1)S(1)}, bf16[128,1024]{1,0:T(8,128)(2,1)}, u32[]{:S(2)}, u32[]{:S(2)}) collective-permute-start(bf16[128,1024]{1,0:T(8,128)(2,1)S(1)} %get-tuple-element.13), channel_id=1, source_target_pairs={{1,0},{2,1},{3,2},{0,3},{5,4},{6,5},{7,6},{4,7},{9,8},{10,9},{11,1... | collective-permute-start | bytes 786440 | tf_op jit(solution)/shard_map/ppermute | solution.py:13
  200.8 9.1 %collective-permute-start.9 = (bf16[128,1024]{1,0:T(8,128)(2,1)}, bf16[128,1024]{1,0:T(8,128)(2,1)}, u32[]{:S(2)}, u32[]{:S(2)}) collective-permute-start(bf16[128,1024]{1,0:T(8,128)(2,1)} %get-tuple-element.12), channel_id=1, source_target_pairs={{2,0},{3,1},{0,2},{1,3},{6,4},{7,5},{4,6},{5,7},{10,8},{11,9},{8,1... | collective-permute-start | bytes 786440 | tf_op jit(solution)/shard_map/ppermute | solution.py:13
  202.3 14.3 %collective-permute-start.10 = (bf16[128,1024]{1,0:T(8,128)(2,1)S(1)}, bf16[128,1024]{1,0:T(8,128)(2,1)}, u32[]{:S(2)}, u32[]{:S(2)}) collective-permute-start(bf16[128,1024]{1,0:T(8,128)(2,1)S(1)} %get-tuple-element.11), channel_id=1, source_target_pairs={{3,0},{0,1},{1,2},{2,3},{7,4},{4,5},{5,6},{6,7},{11,8},{8,9},{9,10... | collective-permute-start | bytes 786440 | tf_op jit(solution)/shard_map/ppermute | solution.py:13
  (9 other events, 16.3 us)
Sparse Core Ops, SparseCore 0:
  78.1 39.1 all-gather.1
  154.1 32.8 reduce-scatter.1

commit v2 on v0

v2 whole, which is shorter than its diff:
```python
import jax
import jax.numpy as jnp
from jax import lax
from jax.experimental import pallas as pl
from jax.experimental.pallas import tpu as pltpu
from jax.sharding import Mesh, PartitionSpec as P

AXES = ("ylo", "z", "core", "yhi", "x")
SIZES = (2, 8, 2, 2, 4)
F32 = jnp.float32
BF16 = jnp.bfloat16
VMEM = pltpu.CompilerParams(vmem_limit_bytes=32 * 1024 * 1024)


def from_x(value, offset):
    return lax.ppermute(value, "x", [((i + offset) % 4, i) for i in range(4)])


def swap(value, axis):
    return lax.ppermute(value, axis, [(0, 1), (1, 0)])


def rank16(ylo, core, x):
    return (ylo * 2 + core) * 4 + x


def owner_pairs(flip):
    return [
        (rank16(ylo, core, x), rank16(x % 2, x // 2, (x + core + 2 * (ylo ^ flip)) % 4))
        for ylo in range(2)
        for core in range(2)
        for x in range(4)
    ]


def to_owner(value, flip):
    return lax.ppermute(value, ("ylo", "core", "x"), owner_pairs(flip))


def from_owner(value, flip):
    return lax.ppermute(value, ("ylo", "core", "x"), [(b, a) for a, b in owner_pairs(flip)])


barrier = lax.optimization_barrier


def dot(a, b, ca, cb):
    return lax.dot_general(a, b, (((ca,), (cb,)), ((), ())), preferred_element_type=F32)


ORDER = (4, 3, 5, 2, 6, 1, 7, 0)


def along_z(value, offset):
    return lax.ppermute(value, "z", [(i, (i + offset) % 8) for i in range(8)])


def lanes(pos_ref, block, place):
    z = lax.rem(pos_ref[0] + ORDER[place], 8)
    return pl.ds(pl.multiple_of(((block % 2) * 16 + z * 2 + block // 2) * 128, 128), 128)


def split_body(pos_ref, acts_ref, out_ref):
    for block in range(4):
        for place in range(8):
            out_ref[block * 128 : (block + 1) * 128, place * 128 : (place + 1) * 128] = acts_ref[:, lanes(pos_ref, block, place)]


def merge_body(pos_ref, parts_ref, out_ref):
    for block in range(4):
        rows = pl.ds(block * 128, 128)
        for place in range(8):
            cols = pl.ds(place * 128, 128)
            total = parts_ref[0, rows, cols].astype(F32) + parts_ref[1, rows, cols].astype(F32)
            out_ref[:, lanes(pos_ref, block, place)] = total


def local_call(body, pos, arg, shape, dtype):
    return pl.pallas_call(
        body,
        in_specs=[pl.BlockSpec(memory_space=pltpu.SMEM), pl.BlockSpec(memory_space=pltpu.VMEM)],
        out_specs=pl.BlockSpec(memory_space=pltpu.VMEM),
        out_shape=jax.ShapeDtypeStruct(shape, dtype),
        compiler_params=VMEM,
    )(pos, arg)


def per_device(acts, grad_out, weight):
    ylo, core = lax.axis_index("ylo"), lax.axis_index("core")
    yhi = lax.axis_index("yhi")
    pos = lax.axis_index("z").reshape(1)

    w_a, w_b = from_owner(weight, 0), from_owner(weight, 1)
    split = local_call(split_body, pos, acts, (512, 1024), BF16)
    split, w_a, w_b = barrier((split, w_a, w_b))
    w = jnp.concatenate([jnp.where(ylo == 0, w_a, w_b), jnp.where(ylo == 0, w_b, w_a)], axis=1)
    shards = {0: w}

    def gather_step(step):
        shards[step] = along_z(shards[step - 1], -1)
        shards[8 - step] = along_z(shards[(9 - step) % 8], 1)

    half = lax.all_to_all(split, "x", 0, 0, tiled=True)
    gather_step(1)
    g0, half, shards[1], shards[7] = barrier((grad_out, half, shards[1], shards[7]))

    g1, g3 = from_x(g0, 1), from_x(g0, -1)
    other = swap(half, "yhi")
    gather_step(2)
    gather_step(3)
    g1, g3, other, shards[3], shards[5] = barrier((g1, g3, other, shards[3], shards[5]))

    g2 = (from_x(g1[:512], 1), from_x(g3[512:], -1))
    last = (along_z(shards[3][:64], -1), along_z(shards[5][64:], 1))
    g2, last = barrier((g2, last))
    g2 = jnp.concatenate(g2)
    shards[4] = jnp.concatenate(last)
    w_own = jnp.concatenate([shards[place] for place in ORDER])
    tokens = jnp.zeros((2, 512, 1024), BF16)
    tokens = lax.dynamic_update_index_in_dim(tokens, half, yhi, 0)
    tokens = lax.dynamic_update_index_in_dim(tokens, other, 1 - yhi, 0)
    tokens = tokens.reshape(1024, 1024)

    first = core == 0
    g_all_own = jnp.concatenate([jnp.where(first, g0, g1), jnp.where(first, g2, g3)], axis=1)
    g_all_other = jnp.concatenate([jnp.where(first, g1, g0), jnp.where(first, g3, g2)], axis=1)

    def term(start, stop):
        rows = tokens[:, start * 128 : stop * 128]
        give = swap(dot(rows, g_all_other, 0, 0).astype(BF16), "core")
        return dot(rows, g_all_own, 0, 0) + give.astype(F32)

    far = term(0, 3)
    near = term(3, 8)
    blocks = [far[:128], far[128:256], far[256:]] + [near[i * 128 : (i + 1) * 128] for i in range(5)]
    blocks = dict(zip(ORDER, blocks))

    def sent(value, offset):
        return along_z(value.astype(BF16), offset)

    via = (sent(blocks[3], 1), sent(blocks[5], -1), sent(blocks[4][:64], 2), sent(blocks[4][64:], -2))
    w_other = swap(w_own, "core")
    part = [
        (dot(g_all_own[rows], w_own, 1, 1) + dot(g_all_other[rows], w_other, 1, 1)).astype(BF16)
        for rows in (slice(0, 512), slice(512, 1024))
    ]
    via, part = barrier((via, part))
    via_up, via_down, via_up2, via_down2 = [v.astype(F32) for v in via]
    up = blocks[2] + via_up
    down = blocks[6] + via_down
    up = sent(jnp.concatenate([up[:64] + via_up2, up[64:]]), 2)
    down = sent(jnp.concatenate([down[:64], down[64:] + via_down2]), -2)
    near = (sent(blocks[1], 1), sent(blocks[7], -1))
    sums = blocks[0]
    for value in (up, down, *near):
        sums = sums + value.astype(F32)
    sums = sums.astype(BF16)
    low, high = sums[:, :512], sums[:, 512:]
    here = to_owner(jnp.where(ylo == 0, low, high), 0)
    there = to_owner(jnp.where(ylo == 0, high, low), 1)
    grad_weight = (here.astype(F32) + there.astype(F32)) / jnp.sqrt(F32(32768))

    parts = lax.all_to_all(jnp.concatenate(part), ("yhi", "x"), 0, 0, tiled=True).reshape(2, 512, 1024)
    grad_acts = local_call(merge_body, pos, parts, (128, 4096), F32)
    return (grad_acts, grad_weight)


def solution(mesh):
    fine = Mesh(mesh.devices.reshape(SIZES), AXES)
    rows = P(AXES, None)
    blocks = P(("ylo", "z", "core"), ("yhi", "x"))
    return jax.shard_map(
        per_device,
        mesh=fine,
        in_specs=(rows, blocks, blocks),
        out_specs=(rows, blocks),
        check_vma=False,
    )
```

time: 456 us -> 147 us (0.32)
  waiting for transfers between devices: 412 us -> 52.4 us
  starting transfers between devices: 0.16 us -> 63.3 us
  between operations: 13.8 us -> 1.08 us
  local copies, waits for them, and re-layouts: 0.01 us -> 6.64 us
  matrix products: 17.3 us -> 11.8 us
    reduce_scatter x2 -> x0, waiting for transfers between devices: 232 us -> none  [the longest x1 123 us: per_device(): lax.psum_scatter(local_term, 'dp', scatter_dimension=0, tiled=True)]
    all_gather x2 -> x0, waiting for transfers between devices: 179 us -> none  [the longest x1 106 us: per_device(): gathered = lax.all_gather(acts, 'seq', axis=0, tiled=True)]
    ppermute x0 -> x28, starting transfers between devices: none -> 55.8 us  [the longest x16 26.9 us: along_z(): return lax.ppermute(value, 'z', [(i, (i + offset) % 8) for i in range(8)])]
    ppermute x0 -> x28, waiting for transfers between devices: none -> 52.4 us  [the longest x16 35 us: along_z(): return lax.ppermute(value, 'z', [(i, (i + offset) % 8) for i in range(8)])]
    all_to_all x0 -> x2, starting transfers between devices: none -> 7.42 us  [the longest x1 3.91 us: per_device(): lax.all_to_all(jnp.concatenate(part), ('yhi', 'x'), 0, 0, tiled=True)]
    convert_element_type x2 -> x1, other arithmetic: 7.18 us -> 1.24 us  [per_device(): sums = sums.astype(BF16)]
    dot_general x2 -> x8, matrix products: 17.3 us -> 11.8 us  [dot(): lax.dot_general(a, b, (((ca,), (cb,)), ((), ())), preferred_element_type=...]
  transfers between devices with their start and end apart: 4 -> 30, of which waited for: 4 -> 15; matrix products, arithmetic and copies ran while one was open for 5% -> 15% of each run, Pallas kernels for 0% -> 1%
where the time goes in v2:
time: 147 us; the launch traced here: 145 us
  starting transfers between devices  63.3 us (43%)
  waiting for transfers between devices  52.4 us (36%)
  matrix products  11.8 us (8%)
  local copies, waits for them, and re-layouts  6.64 us (5%)
  other arithmetic  6.63 us (5%)
  Pallas kernels  2.87 us (2%)
    ppermute x16, waiting for transfers between devices, along_z(): return lax.ppermute(value, 'z', [(i, (i + offset) % 8) for i in range(8)])  35 us
    ppermute x16, starting transfers between devices, along_z(): return lax.ppermute(value, 'z', [(i, (i + offset) % 8) for i in range(8)])  26.9 us
    dot_general x8, matrix products, dot(): lax.dot_general(a, b, (((ca,), (cb,)), ((), ())), preferred_element_type=...  11.8 us
    ppermute x2, starting transfers between devices, from_owner(): lax.ppermute(value, ('ylo', 'core', 'x'), [(b, a) for a, b in owner_pairs...  9.47 us
    ppermute x4, waiting for transfers between devices, from_x(): return lax.ppermute(value, 'x', [((i + offset) % 4, i) for i in range(4)])  7.74 us
    ppermute x2, starting transfers between devices, to_owner(): return lax.ppermute(value, ('ylo', 'core', 'x'), owner_pairs(flip))  7.32 us
    ppermute x4, starting transfers between devices, swap(): return lax.ppermute(value, axis, [(0, 1), (1, 0)])  6.8 us
    ppermute x2, waiting for transfers between devices, to_owner(): return lax.ppermute(value, ('ylo', 'core', 'x'), owner_pairs(flip))  6.76 us
  transfers between devices with their start and end apart: 30, of which 15 were waited for; matrix products, arithmetic and copies ran while one was open for 15% of the time, Pallas kernels for 1%

profile of v2, /device:TPU:1, one launch (start us, length us, event | category | flops | bytes accessed | tf_op | source)
XLA Modules:
  0.0 144.7 jit_solution(7917121716813247141)
XLA Ops:
  0.6 7.1 %collective-permute-start = (bf16[128,512]{1,0:T(8,128)(2,1)}, bf16[128,512]{1,0:T(8,128)(2,1)S(1)}, u32[]{:S(2)}, u32[]{:S(2)}) collective-permute-start(bf16[128,512]{1,0:T(8,128)(2,1)} %param.5), channel_id=1, source_target_pairs={{0,0},{129,1},{10,2},{139,3},{1,8},{130,9},{11,10},{136,11},{2,128... | collective-permute-start | bytes 393224 | tf_op jit(solution)/shard_map/ppermute | solution.py:41
  12.6 2.8 %collective-permute-done.1 = bf16[128,512]{1,0:T(8,128)(2,1)S(1)} collective-permute-done((bf16[128,512]{1,0:T(8,128)(2,1)}, bf16[128,512]{1,0:T(8,128)(2,1)S(1)}, u32[]{:S(2)}, u32[]{:S(2)}) %collective-permute-start.1) | collective-permute-done | bytes 131104 | tf_op jit(solution)/shard_map/ppermute | solution.py:41
  15.4 3.5 %all-to-all-start = ((bf16[4,128,1024]{2,1,0:T(8,128)(2,1)}), bf16[4,128,1024]{2,1,0:T(8,128)(2,1)S(1)}, u32[]{:S(2)}, u32[]{:S(2)}) async-start(bf16[4,128,1024]{2,1,0:T(8,128)(2,1)} %bitcast.1), calls=%async_computation | async-start | bytes 2097152 | tf_op jit(solution)/shard_map/all_to_all | solution.py:103
  19.0 5.7 %collective-permute-start.2 = (bf16[128,1024]{1,0:T(8,128)(2,1)S(1)}, bf16[128,1024]{1,0:T(8,128)(2,1)S(1)}, u32[]{:S(2)}, u32[]{:S(2)}) collective-permute-start(bf16[128,1024]{1,0:T(8,128)(2,1)S(1)} %pad_maximum_fusion.11), channel_id=1, source_target_pairs={{0,112},{16,0},{32,16},{48,32},{64,48},{80,64},{96,80},{112,96},{1... | collective-permute-start | bytes 786440 | tf_op jit(solution)/shard_map/ppermute | solution.py:55
  24.6 5.7 %collective-permute-done.2 = bf16[128,1024]{1,0:T(8,128)(2,1)S(1)} collective-permute-done((bf16[128,1024]{1,0:T(8,128)(2,1)S(1)}, bf16[128,1024]{1,0:T(8,128)(2,1)S(1)}, u32[]{:S(2)}, u32[]{:S(2)}) %collective-permute-start.2) | collective-permute-done | bytes 262176 | tf_op jit(solution)/shard_map/ppermute | solution.py:55
  30.3 3.5 %collective-permute-done.3 = bf16[128,1024]{1,0:T(8,128)(2,1)S(1)} collective-permute-done((bf16[128,1024]{1,0:T(8,128)(2,1)S(1)}, bf16[128,1024]{1,0:T(8,128)(2,1)S(1)}, u32[]{:S(2)}, u32[]{:S(2)}) %collective-permute-start.3) | collective-permute-done | bytes 262176 | tf_op jit(solution)/shard_map/ppermute | solution.py:55
  34.5 2.8 %collective-permute-start.4 = (bf16[1024,512]{1,0:T(8,128)(2,1)}, bf16[1024,512]{1,0:T(8,128)(2,1)S(1)}, u32[]{:S(2)}, u32[]{:S(2)}) collective-permute-start(bf16[1024,512]{1,0:T(8,128)(2,1)} %param.4), channel_id=1, source_target_pairs={{1,0},{2,1},{3,2},{0,3},{5,4},{6,5},{7,6},{4,7},{9,8},{10,9},{11,1... | collective-permute-start | bytes 3145736 | tf_op jit(solution)/shard_map/ppermute | solution.py:16
  37.4 2.6 %collective-permute-start.6 = (bf16[512,1024]{1,0:T(8,128)(2,1)S(1)}, bf16[512,1024]{1,0:T(8,128)(2,1)}, u32[]{:S(2)}, u32[]{:S(2)}) collective-permute-start(bf16[512,1024]{1,0:T(8,128)(2,1)S(1)} %bitcast.16), channel_id=1, source_target_pairs={{0,4},{4,0},{1,5},{5,1},{2,6},{6,2},{3,7},{7,3},{8,12},{12,8},{9,1... | collective-permute-start | bytes 3145736 | tf_op jit(solution)/shard_map/ppermute | solution.py:20
  40.0 3.5 %collective-permute-start.7 = (bf16[128,1024]{1,0:T(8,128)(2,1)}, bf16[128,1024]{1,0:T(8,128)(2,1)}, u32[]{:S(2)}, u32[]{:S(2)}) collective-permute-start(bf16[128,1024]{1,0:T(8,128)(2,1)} %copy-done.1), channel_id=1, source_target_pairs={{0,112},{16,0},{32,16},{48,32},{64,48},{80,64},{96,80},{112,96},{1... | collective-permute-start | bytes 786440 | tf_op jit(solution)/shard_map/ppermute | solution.py:55
  43.5 4.7 %collective-permute-done.7 = bf16[128,1024]{1,0:T(8,128)(2,1)} collective-permute-done((bf16[128,1024]{1,0:T(8,128)(2,1)}, bf16[128,1024]{1,0:T(8,128)(2,1)}, u32[]{:S(2)}, u32[]{:S(2)}) %collective-permute-start.7) | collective-permute-done | bytes 262176 | tf_op jit(solution)/shard_map/ppermute | solution.py:55
  48.2 3.4 %collective-permute-start.8 = (bf16[128,1024]{1,0:T(8,128)(2,1)}, bf16[128,1024]{1,0:T(8,128)(2,1)S(1)}, u32[]{:S(2)}, u32[]{:S(2)}) collective-permute-start(bf16[128,1024]{1,0:T(8,128)(2,1)} %collective-permute-done.7), channel_id=1, source_target_pairs={{0,112},{16,0},{32,16},{48,32},{64,48},{80,64},{96,80},{112,96},{1... | collective-permute-start | bytes 786440 | tf_op jit(solution)/shard_map/ppermute | solution.py:55
  52.0 3.4 %collective-permute-done.8 = bf16[128,1024]{1,0:T(8,128)(2,1)S(1)} collective-permute-done((bf16[128,1024]{1,0:T(8,128)(2,1)}, bf16[128,1024]{1,0:T(8,128)(2,1)S(1)}, u32[]{:S(2)}, u32[]{:S(2)}) %collective-permute-start.8) | collective-permute-done | bytes 262176 | tf_op jit(solution)/shard_map/ppermute | solution.py:55
  55.4 3.3 %collective-permute-done.10 = bf16[128,1024]{1,0:T(8,128)(2,1)S(1)} collective-permute-done((bf16[128,1024]{1,0:T(8,128)(2,1)}, bf16[128,1024]{1,0:T(8,128)(2,1)S(1)}, u32[]{:S(2)}, u32[]{:S(2)}) %collective-permute-start.10) | collective-permute-done | bytes 262176 | tf_op jit(solution)/shard_map/ppermute | solution.py:55
  59.7 3.1 %collective-permute-done.5 = bf16[1024,512]{1,0:T(8,128)(2,1)S(1)} collective-permute-done((bf16[1024,512]{1,0:T(8,128)(2,1)}, bf16[1024,512]{1,0:T(8,128)(2,1)S(1)}, u32[]{:S(2)}, u32[]{:S(2)}) %collective-permute-start.5) | collective-permute-done | bytes 1048608 | tf_op jit(solution)/shard_map/ppermute | solution.py:16
  65.5 3.2 %collective-permute-start.13 = (bf16[64,1024]{1,0:T(8,128)(2,1)S(1)}, bf16[64,1024]{1,0:T(8,128)(2,1)S(1)}, u32[]{:S(2)}, u32[]{:S(2)}) collective-permute-start(bf16[64,1024]{1,0:T(8,128)(2,1)S(1)} %slice.89), channel_id=1, source_target_pairs={{0,112},{16,0},{32,16},{48,32},{64,48},{80,64},{96,80},{112,96},{1... | collective-permute-start | bytes 393224 | tf_op jit(solution)/shard_map/ppermute | solution.py:55
  74.7 3.1 %collective-permute-done.12 = bf16[512,512]{1,0:T(8,128)(2,1)S(1)} collective-permute-done((bf16[512,512]{1,0:T(8,128)(2,1)S(1)}, bf16[512,512]{1,0:T(8,128)(2,1)S(1)}, u32[]{:S(2)}, u32[]{:S(2)}) %collective-permute-start.12) | collective-permute-done | bytes 524320 | tf_op jit(solution)/shard_map/ppermute | solution.py:16
  79.0 3.5 %collective-permute-start.15 = (bf16[384,1024]{1,0:T(8,128)(2,1)S(1)}, bf16[384,1024]{1,0:T(8,128)(2,1)S(1)}, u32[]{:S(2)}, u32[]{:S(2)}) collective-permute-start(bf16[384,1024]{1,0:T(8,128)(2,1)S(1)} %convolution_convert_fusion.1), channel_id=1, source_target_pairs={{0,8},{8,0},{1,9},{9,1},{2,10},{10,2},{3,11},{11,3},{4,12},{12,4},... | collective-permute-start | bytes 2359304 | tf_op jit(solution)/shard_map/ppermute | solution.py:20
  88.1 3.2 %collective-permute-start.17 = (bf16[128,1024]{1,0:T(8,128)(2,1)S(1)}, bf16[128,1024]{1,0:T(8,128)(2,1)S(1)}, u32[]{:S(2)}, u32[]{:S(2)}) collective-permute-start(bf16[128,1024]{1,0:T(8,128)(2,1)S(1)} %get-tuple-element.56), channel_id=1, source_target_pairs={{0,112},{16,0},{32,16},{48,32},{64,48},{80,64},{96,80},{112,96},{1... | collective-permute-start | bytes 786440 | tf_op jit(solution)/shard_map/ppermute | solution.py:55
  91.4 3.6 %collective-permute-start.19 = (bf16[64,1024]{1,0:T(8,128)(2,1)S(1)}, bf16[64,1024]{1,0:T(8,128)(2,1)S(1)}, u32[]{:S(2)}, u32[]{:S(2)}) collective-permute-start(bf16[64,1024]{1,0:T(8,128)(2,1)S(1)} %get-tuple-element.54), channel_id=1, source_target_pairs={{0,96},{16,112},{32,0},{48,16},{64,32},{80,48},{96,64},{112,80},{1... | collective-permute-start | bytes 393224 | tf_op jit(solution)/shard_map/ppermute | solution.py:55
  94.9 3.1 %fusion.33 = (bf16[640,1024]{1,0:T(8,128)(2,1)S(1)}, f32[640,1024]{1,0:T(8,128)}) fusion(bf16[640,1024]{1,0:T(8,128)(2,1)S(1)} %collective-permute-done.21, bf16[1024,512]{1,0:T(8,128)(2,1)S(1)} %get-tuple-element.50, bf16[1024,512]{1,0:T(8,128)(2,1)S(1)} %get-tuple-element.48, bf16[1024,1024]{1,0:T(8,128)(2,1)S(1)} %bitcast.21), kind=kOutput, calls=%fused_computation.78 | convolution fusion | flops 1348337664 | bytes 8650752 | tf_op jit(solution)/shard_map/dot_general | solution.py:48
  107.1 3.9 %all-to-all-start.1 = ((bf16[8,128,1024]{2,1,0:T(8,128)(2,1)}), bf16[8,128,1024]{2,1,0:T(8,128)(2,1)S(1)}, u32[]{:S(2)}, u32[]{:S(2)}) async-start(bf16[8,128,1024]{2,1,0:T(8,128)(2,1)} %bitcast.15), calls=%async_computation.1 | async-start | bytes 4194304 | tf_op jit(solution)/shard_map/all_to_all | solution.py:163
  115.1 11.9 %collective-permute-done.23 = bf16[128,1024]{1,0:T(8,128)(2,1)S(1)} collective-permute-done((bf16[128,1024]{1,0:T(8,128)(2,1)S(1)}, bf16[128,1024]{1,0:T(8,128)(2,1)S(1)}, u32[]{:S(2)}, u32[]{:S(2)}) %collective-permute-start.23) | collective-permute-done | bytes 262176 | tf_op jit(solution)/shard_map/ppermute | solution.py:55
  128.2 5.4 %collective-permute-start.27 = (bf16[128,512]{1,0:T(8,128)(2,1)S(1)}, bf16[128,512]{1,0:T(8,128)(2,1)S(1)}, u32[]{:S(2)}, u32[]{:S(2)}) collective-permute-start(bf16[128,512]{1,0:T(8,128)(2,1)S(1)} %get-tuple-element.59), channel_id=1, source_target_pairs={{0,2},{1,131},{2,8},{3,137},{8,3},{9,128},{10,9},{11,138},{128,0},... | collective-permute-start | bytes 393224 | tf_op jit(solution)/shard_map/ppermute | solution.py:37
  135.5 5.3 %collective-permute-done.27 = bf16[128,512]{1,0:T(8,128)(2,1)S(1)} collective-permute-done((bf16[128,512]{1,0:T(8,128)(2,1)S(1)}, bf16[128,512]{1,0:T(8,128)(2,1)S(1)}, u32[]{:S(2)}, u32[]{:S(2)}) %collective-permute-start.27) | collective-permute-done | bytes 131104 | tf_op jit(solution)/shard_map/ppermute | solution.py:37
  (96 shorter events, 42.5 us)
Async XLA Ops:
  0.6 12.0 %collective-permute-start = (bf16[128,512]{1,0:T(8,128)(2,1)}, bf16[128,512]{1,0:T(8,128)(2,1)S(1)}, u32[]{:S(2)}, u32[]{:S(2)}) collective-permute-start(bf16[128,512]{1,0:T(8,128)(2,1)} %param.5), channel_id=1, source_target_pairs={{0,0},{129,1},{10,2},{139,3},{1,8},{130,9},{11,10},{136,11},{2,128... | collective-permute-start | bytes 393224 | tf_op jit(solution)/shard_map/ppermute | solution.py:41
  15.4 18.4 %all-to-all-start = ((bf16[4,128,1024]{2,1,0:T(8,128)(2,1)}), bf16[4,128,1024]{2,1,0:T(8,128)(2,1)S(1)}, u32[]{:S(2)}, u32[]{:S(2)}) async-start(bf16[4,128,1024]{2,1,0:T(8,128)(2,1)} %bitcast.1), calls=%async_computation | async-start | bytes 2097152 | tf_op jit(solution)/shard_map/all_to_all | solution.py:103
  19.0 11.3 %collective-permute-start.2 = (bf16[128,1024]{1,0:T(8,128)(2,1)S(1)}, bf16[128,1024]{1,0:T(8,128)(2,1)S(1)}, u32[]{:S(2)}, u32[]{:S(2)}) collective-permute-start(bf16[128,1024]{1,0:T(8,128)(2,1)S(1)} %pad_maximum_fusion.11), channel_id=1, source_target_pairs={{0,112},{16,0},{32,16},{48,32},{64,48},{80,64},{96,80},{112,96},{1... | collective-permute-start | bytes 786440 | tf_op jit(solution)/shard_map/ppermute | solution.py:55
  24.6 9.2 %collective-permute-start.3 = (bf16[128,1024]{1,0:T(8,128)(2,1)S(1)}, bf16[128,1024]{1,0:T(8,128)(2,1)S(1)}, u32[]{:S(2)}, u32[]{:S(2)}) collective-permute-start(bf16[128,1024]{1,0:T(8,128)(2,1)S(1)} %pad_maximum_fusion.11), channel_id=1, source_target_pairs={{0,16},{16,32},{32,48},{48,64},{64,80},{80,96},{96,112},{112,0},{1... | collective-permute-start | bytes 786440 | tf_op jit(solution)/shard_map/ppermute | solution.py:55
  34.5 25.1 %collective-permute-start.4 = (bf16[1024,512]{1,0:T(8,128)(2,1)}, bf16[1024,512]{1,0:T(8,128)(2,1)S(1)}, u32[]{:S(2)}, u32[]{:S(2)}) collective-permute-start(bf16[1024,512]{1,0:T(8,128)(2,1)} %param.4), channel_id=1, source_target_pairs={{1,0},{2,1},{3,2},{0,3},{5,4},{6,5},{7,6},{4,7},{9,8},{10,9},{11,1... | collective-permute-start | bytes 3145736 | tf_op jit(solution)/shard_map/ppermute | solution.py:16
  37.4 25.4 %collective-permute-start.5 = (bf16[1024,512]{1,0:T(8,128)(2,1)}, bf16[1024,512]{1,0:T(8,128)(2,1)S(1)}, u32[]{:S(2)}, u32[]{:S(2)}) collective-permute-start(bf16[1024,512]{1,0:T(8,128)(2,1)} %param.4), channel_id=1, source_target_pairs={{3,0},{0,1},{1,2},{2,3},{7,4},{4,5},{5,6},{6,7},{11,8},{8,9},{9,10... | collective-permute-start | bytes 3145736 | tf_op jit(solution)/shard_map/ppermute | solution.py:16
  37.4 25.5 %collective-permute-start.6 = (bf16[512,1024]{1,0:T(8,128)(2,1)S(1)}, bf16[512,1024]{1,0:T(8,128)(2,1)}, u32[]{:S(2)}, u32[]{:S(2)}) collective-permute-start(bf16[512,1024]{1,0:T(8,128)(2,1)S(1)} %bitcast.16), channel_id=1, source_target_pairs={{0,4},{4,0},{1,5},{5,1},{2,6},{6,2},{3,7},{7,3},{8,12},{12,8},{9,1... | collective-permute-start | bytes 3145736 | tf_op jit(solution)/shard_map/ppermute | solution.py:20
  40.0 8.2 %collective-permute-start.7 = (bf16[128,1024]{1,0:T(8,128)(2,1)}, bf16[128,1024]{1,0:T(8,128)(2,1)}, u32[]{:S(2)}, u32[]{:S(2)}) collective-permute-start(bf16[128,1024]{1,0:T(8,128)(2,1)} %copy-done.1), channel_id=1, source_target_pairs={{0,112},{16,0},{32,16},{48,32},{64,48},{80,64},{96,80},{112,96},{1... | collective-permute-start | bytes 786440 | tf_op jit(solution)/shard_map/ppermute | solution.py:55
  43.5 8.1 %collective-permute-start.9 = (bf16[128,1024]{1,0:T(8,128)(2,1)}, bf16[128,1024]{1,0:T(8,128)(2,1)}, u32[]{:S(2)}, u32[]{:S(2)}) collective-permute-start(bf16[128,1024]{1,0:T(8,128)(2,1)} %copy-done.3), channel_id=1, source_target_pairs={{0,16},{16,32},{32,48},{48,64},{64,80},{80,96},{96,112},{112,0},{1... | collective-permute-start | bytes 786440 | tf_op jit(solution)/shard_map/ppermute | solution.py:55
  62.9 11.8 %collective-permute-start.11 = (bf16[512,512]{1,0:T(8,128)(2,1)S(1)}, bf16[512,512]{1,0:T(8,128)(2,1)S(1)}, u32[]{:S(2)}, u32[]{:S(2)}) collective-permute-start(bf16[512,512]{1,0:T(8,128)(2,1)S(1)} %slice.87), channel_id=1, source_target_pairs={{1,0},{2,1},{3,2},{0,3},{5,4},{6,5},{7,6},{4,7},{9,8},{10,9},{11,1... | collective-permute-start | bytes 1572872 | tf_op jit(solution)/shard_map/ppermute | solution.py:16
  65.4 12.4 %collective-permute-start.12 = (bf16[512,512]{1,0:T(8,128)(2,1)S(1)}, bf16[512,512]{1,0:T(8,128)(2,1)S(1)}, u32[]{:S(2)}, u32[]{:S(2)}) collective-permute-start(bf16[512,512]{1,0:T(8,128)(2,1)S(1)} %slice.88), channel_id=1, source_target_pairs={{3,0},{0,1},{1,2},{2,3},{7,4},{4,5},{5,6},{6,7},{11,8},{8,9},{9,10... | collective-permute-start | bytes 1572872 | tf_op jit(solution)/shard_map/ppermute | solution.py:16
  79.0 7.9 %collective-permute-start.15 = (bf16[384,1024]{1,0:T(8,128)(2,1)S(1)}, bf16[384,1024]{1,0:T(8,128)(2,1)S(1)}, u32[]{:S(2)}, u32[]{:S(2)}) collective-permute-start(bf16[384,1024]{1,0:T(8,128)(2,1)S(1)} %convolution_convert_fusion.1), channel_id=1, source_target_pairs={{0,8},{8,0},{1,9},{9,1},{2,10},{10,2},{3,11},{11,3},{4,12},{12,4},... | collective-permute-start | bytes 2359304 | tf_op jit(solution)/shard_map/ppermute | solution.py:20
  84.7 14.1 %collective-permute-start.20 = (bf16[1024,1024]{1,0:T(8,128)(2,1)S(1)}, bf16[1024,1024]{1,0:T(8,128)(2,1)S(1)}, u32[]{:S(2)}, u32[]{:S(2)}) collective-permute-start(bf16[1024,1024]{1,0:T(8,128)(2,1)S(1)} %constant_dynamic-update-slice_fusion.2), channel_id=1, source_target_pairs={{0,8},{8,0},{1,9},{9,1},{2,10},{10,2},{3,11},{11,3},{4,12},{12,4},... | collective-permute-start | bytes 6291464 | tf_op jit(solution)/shard_map/ppermute | solution.py:20
  88.0 17.5 %collective-permute-start.16 = (bf16[128,1024]{1,0:T(8,128)(2,1)S(1)}, bf16[128,1024]{1,0:T(8,128)(2,1)S(1)}, u32[]{:S(2)}, u32[]{:S(2)}) collective-permute-start(bf16[128,1024]{1,0:T(8,128)(2,1)S(1)} %get-tuple-element.57), channel_id=1, source_target_pairs={{0,16},{16,32},{32,48},{48,64},{64,80},{80,96},{96,112},{112,0},{1... | collective-permute-start | bytes 786440 | tf_op jit(solution)/shard_map/ppermute | solution.py:55
  88.1 17.4 %collective-permute-start.17 = (bf16[128,1024]{1,0:T(8,128)(2,1)S(1)}, bf16[128,1024]{1,0:T(8,128)(2,1)S(1)}, u32[]{:S(2)}, u32[]{:S(2)}) collective-permute-start(bf16[128,1024]{1,0:T(8,128)(2,1)S(1)} %get-tuple-element.56), channel_id=1, source_target_pairs={{0,112},{16,0},{32,16},{48,32},{64,48},{80,64},{96,80},{112,96},{1... | collective-permute-start | bytes 786440 | tf_op jit(solution)/shard_map/ppermute | solution.py:55
  91.3 12.8 %collective-permute-start.18 = (bf16[64,1024]{1,0:T(8,128)(2,1)S(1)}, bf16[64,1024]{1,0:T(8,128)(2,1)S(1)}, u32[]{:S(2)}, u32[]{:S(2)}) collective-permute-start(bf16[64,1024]{1,0:T(8,128)(2,1)S(1)} %get-tuple-element.55), channel_id=1, source_target_pairs={{0,32},{16,48},{32,64},{48,80},{64,96},{80,112},{96,0},{112,16},{1... | collective-permute-start | bytes 393224 | tf_op jit(solution)/shard_map/ppermute | solution.py:55
  91.4 14.1 %collective-permute-start.19 = (bf16[64,1024]{1,0:T(8,128)(2,1)S(1)}, bf16[64,1024]{1,0:T(8,128)(2,1)S(1)}, u32[]{:S(2)}, u32[]{:S(2)}) collective-permute-start(bf16[64,1024]{1,0:T(8,128)(2,1)S(1)} %get-tuple-element.54), channel_id=1, source_target_pairs={{0,96},{16,112},{32,0},{48,16},{64,32},{80,48},{96,64},{112,80},{1... | collective-permute-start | bytes 393224 | tf_op jit(solution)/shard_map/ppermute | solution.py:55
  98.7 16.3 %collective-permute-start.25 = (bf16[128,1024]{1,0:T(8,128)(2,1)}, bf16[128,1024]{1,0:T(8,128)(2,1)S(1)}, u32[]{:S(2)}, u32[]{:S(2)}) collective-permute-start(bf16[128,1024]{1,0:T(8,128)(2,1)} %get-tuple-element.53), channel_id=1, source_target_pairs={{0,112},{16,0},{32,16},{48,32},{64,48},{80,64},{96,80},{112,96},{1... | collective-permute-start | bytes 786440 | tf_op jit(solution)/shard_map/ppermute | solution.py:55
  104.1 11.0 %collective-permute-start.24 = (bf16[128,1024]{1,0:T(8,128)(2,1)S(1)}, bf16[128,1024]{1,0:T(8,128)(2,1)S(1)}, u32[]{:S(2)}, u32[]{:S(2)}) collective-permute-start(bf16[128,1024]{1,0:T(8,128)(2,1)S(1)} %get-tuple-element.52), channel_id=1, source_target_pairs={{0,16},{16,32},{32,48},{48,64},{64,80},{80,96},{96,112},{112,0},{1... | collective-permute-start | bytes 786440 | tf_op jit(solution)/shard_map/ppermute | solution.py:55
  107.1 36.0 %all-to-all-start.1 = ((bf16[8,128,1024]{2,1,0:T(8,128)(2,1)}), bf16[8,128,1024]{2,1,0:T(8,128)(2,1)S(1)}, u32[]{:S(2)}, u32[]{:S(2)}) async-start(bf16[8,128,1024]{2,1,0:T(8,128)(2,1)} %bitcast.15), calls=%async_computation.1 | async-start | bytes 4194304 | tf_op jit(solution)/shard_map/all_to_all | solution.py:163
  112.5 14.5 %collective-permute-start.23 = (bf16[128,1024]{1,0:T(8,128)(2,1)S(1)}, bf16[128,1024]{1,0:T(8,128)(2,1)S(1)}, u32[]{:S(2)}, u32[]{:S(2)}) collective-permute-start(bf16[128,1024]{1,0:T(8,128)(2,1)S(1)} %pad_maximum_fusion.13), channel_id=1, source_target_pairs={{0,96},{16,112},{32,0},{48,16},{64,32},{80,48},{96,64},{112,80},{1... | collective-permute-start | bytes 786440 | tf_op jit(solution)/shard_map/ppermute | solution.py:55
  114.1 12.9 %collective-permute-start.22 = (bf16[128,1024]{1,0:T(8,128)(2,1)S(1)}, bf16[128,1024]{1,0:T(8,128)(2,1)S(1)}, u32[]{:S(2)}, u32[]{:S(2)}) collective-permute-start(bf16[128,1024]{1,0:T(8,128)(2,1)S(1)} %pad_maximum_fusion.12), channel_id=1, source_target_pairs={{0,32},{16,48},{32,64},{48,80},{64,96},{80,112},{96,0},{112,16},{1... | collective-permute-start | bytes 786440 | tf_op jit(solution)/shard_map/ppermute | solution.py:55
  128.2 12.6 %collective-permute-start.27 = (bf16[128,512]{1,0:T(8,128)(2,1)S(1)}, bf16[128,512]{1,0:T(8,128)(2,1)S(1)}, u32[]{:S(2)}, u32[]{:S(2)}) collective-permute-start(bf16[128,512]{1,0:T(8,128)(2,1)S(1)} %get-tuple-element.59), channel_id=1, source_target_pairs={{0,2},{1,131},{2,8},{3,137},{8,3},{9,128},{10,9},{11,138},{128,0},... | collective-permute-start | bytes 393224 | tf_op jit(solution)/shard_map/ppermute | solution.py:37
  133.6 8.7 %collective-permute-start.26 = (bf16[128,512]{1,0:T(8,128)(2,1)S(1)}, bf16[128,512]{1,0:T(8,128)(2,1)S(1)}, u32[]{:S(2)}, u32[]{:S(2)}) collective-permute-start(bf16[128,512]{1,0:T(8,128)(2,1)S(1)} %get-tuple-element.58), channel_id=1, source_target_pairs={{0,0},{1,129},{2,10},{3,139},{8,1},{9,130},{10,11},{11,136},{128,2... | collective-permute-start | bytes 393224 | tf_op jit(solution)/shard_map/ppermute | solution.py:37
  (13 other events, 58.0 us)

commit v3 on v2

--- a/solution.py
+++ b/solution.py
@@ -128,11 +128,10 @@
     def term(start, stop):
         rows = tokens[:, start * 128 : stop * 128]
         give = swap(dot(rows, g_all_other, 0, 0).astype(BF16), "core")
-        return dot(rows, g_all_own, 0, 0) + give.astype(F32)
+        return (dot(rows, g_all_own, 0, 0) + give.astype(F32)).astype(BF16)
 
-    far = term(0, 3)
-    near = term(3, 8)
-    blocks = [far[:128], far[128:256], far[256:]] + [near[i * 128 : (i + 1) * 128] for i in range(5)]
+    whole = term(0, 8)
+    blocks = [whole[i * 128 : (i + 1) * 128] for i in range(8)]
     blocks = dict(zip(ORDER, blocks))
 
     def sent(value, offset):
@@ -140,18 +139,15 @@
 
     via = (sent(blocks[3], 1), sent(blocks[5], -1), sent(blocks[4][:64], 2), sent(blocks[4][64:], -2))
     w_other = swap(w_own, "core")
-    part = [
-        (dot(g_all_own[rows], w_own, 1, 1) + dot(g_all_other[rows], w_other, 1, 1)).astype(BF16)
-        for rows in (slice(0, 512), slice(512, 1024))
-    ]
+    part = dot(jnp.concatenate([g_all_own, g_all_other], axis=1), jnp.concatenate([w_own, w_other], axis=1), 1, 1).astype(BF16)
     via, part = barrier((via, part))
     via_up, via_down, via_up2, via_down2 = [v.astype(F32) for v in via]
-    up = blocks[2] + via_up
-    down = blocks[6] + via_down
+    up = blocks[2].astype(F32) + via_up
+    down = blocks[6].astype(F32) + via_down
     up = sent(jnp.concatenate([up[:64] + via_up2, up[64:]]), 2)
     down = sent(jnp.concatenate([down[:64], down[64:] + via_down2]), -2)
     near = (sent(blocks[1], 1), sent(blocks[7], -1))
-    sums = blocks[0]
+    sums = blocks[0].astype(F32)
     for value in (up, down, *near):
         sums = sums + value.astype(F32)
     sums = sums.astype(BF16)
@@ -160,7 +156,7 @@
     there = to_owner(jnp.where(ylo == 0, high, low), 1)
     grad_weight = (here.astype(F32) + there.astype(F32)) / jnp.sqrt(F32(32768))
 
-    parts = lax.all_to_all(jnp.concatenate(part), ("yhi", "x"), 0, 0, tiled=True).reshape(2, 512, 1024)
+    parts = lax.all_to_all(part, ("yhi", "x"), 0, 0, tiled=True).reshape(2, 512, 1024)
     grad_acts = local_call(merge_body, pos, parts, (128, 4096), F32)
     return (grad_acts, grad_weight)
 

time: 147 us -> 146 us (level); the launches traced: 145 us -> 145 us
    ppermute x2, waiting for transfers between devices: 6.76 us -> 4.65 us  [to_owner(): return lax.ppermute(value, ('ylo', 'core', 'x'), owner_pairs(flip))]
    ppermute x16, starting transfers between devices: 26.9 us -> 28.7 us  [along_z(): return lax.ppermute(value, 'z', [(i, (i + offset) % 8) for i in range(8)])]
    another operation x2, other arithmetic: 0.06 us -> 1.86 us
    ppermute x4, waiting for transfers between devices: 7.74 us -> 9.47 us  [from_x(): return lax.ppermute(value, 'x', [((i + offset) % 4, i) for i in range(4)])]
    concatenate x1 -> x0, other arithmetic: 1.59 us -> none  [per_device(): jnp.concatenate(part)]
    ppermute x4 -> x3, waiting for transfers between devices: 0.09 us -> 1.64 us  [swap(): return lax.ppermute(value, axis, [(0, 1), (1, 0)])]
    dot_general x8 -> x3, matrix products: 11.8 us -> 10.7 us  [dot(): lax.dot_general(a, b, (((ca,), (cb,)), ((), ())), preferred_element_type=...]
    ppermute x4 -> x3, starting transfers between devices: 6.8 us -> 6.04 us  [swap(): return lax.ppermute(value, axis, [(0, 1), (1, 0)])]
  transfers between devices with their start and end apart: 30 -> 29, of which waited for: 15 -> 17; matrix products, arithmetic and copies ran while one was open for 15% -> 13% of each run, Pallas kernels for 1% -> 1%
where the time goes in v3:
time: 146 us; the launch traced here: 145 us
  starting transfers between devices  64.6 us (44%)
  waiting for transfers between devices  53.3 us (37%)
  matrix products  10.7 us (7%)
  local copies, waits for them, and re-layouts  7.25 us (5%)
  other arithmetic  5.66 us (4%)
  Pallas kernels  2.87 us (2%)
    ppermute x16, waiting for transfers between devices, along_z(): return lax.ppermute(value, 'z', [(i, (i + offset) % 8) for i in range(8)])  34.7 us
    ppermute x16, starting transfers between devices, along_z(): return lax.ppermute(value, 'z', [(i, (i + offset) % 8) for i in range(8)])  28.7 us
    dot_general x3, matrix products, dot(): lax.dot_general(a, b, (((ca,), (cb,)), ((), ())), preferred_element_type=...  10.7 us
    ppermute x2, starting transfers between devices, from_owner(): lax.ppermute(value, ('ylo', 'core', 'x'), [(b, a) for a, b in owner_pairs...  9.47 us
    ppermute x4, waiting for transfers between devices, from_x(): return lax.ppermute(value, 'x', [((i + offset) % 4, i) for i in range(4)])  9.47 us
    ppermute x2, starting transfers between devices, to_owner(): return lax.ppermute(value, ('ylo', 'core', 'x'), owner_pairs(flip))  7.6 us
    ppermute x3, starting transfers between devices, swap(): return lax.ppermute(value, axis, [(0, 1), (1, 0)])  6.04 us
    ppermute x4, starting transfers between devices, from_x(): return lax.ppermute(value, 'x', [((i + offset) % 4, i) for i in range(4)])  5.38 us
  transfers between devices with their start and end apart: 29, of which 17 were waited for; matrix products, arithmetic and copies ran while one was open for 13% of the time, Pallas kernels for 1%

profile of v3, /device:TPU:1, one launch (start us, length us, event | category | flops | bytes accessed | tf_op | source)
XLA Modules:
  0.0 145.3 jit_solution(9944763225212822874)
XLA Ops:
  0.6 7.1 %collective-permute-start = (bf16[128,512]{1,0:T(8,128)(2,1)}, bf16[128,512]{1,0:T(8,128)(2,1)S(1)}, u32[]{:S(2)}, u32[]{:S(2)}) collective-permute-start(bf16[128,512]{1,0:T(8,128)(2,1)} %param.5), channel_id=1, source_target_pairs={{0,0},{129,1},{10,2},{139,3},{1,8},{130,9},{11,10},{136,11},{2,128... | collective-permute-start | bytes 393224 | tf_op jit(solution)/shard_map/ppermute | solution.py:41
  12.6 2.8 %collective-permute-done.1 = bf16[128,512]{1,0:T(8,128)(2,1)S(1)} collective-permute-done((bf16[128,512]{1,0:T(8,128)(2,1)}, bf16[128,512]{1,0:T(8,128)(2,1)S(1)}, u32[]{:S(2)}, u32[]{:S(2)}) %collective-permute-start.1) | collective-permute-done | bytes 131104 | tf_op jit(solution)/shard_map/ppermute | solution.py:41
  15.4 3.5 %all-to-all-start = ((bf16[4,128,1024]{2,1,0:T(8,128)(2,1)}), bf16[4,128,1024]{2,1,0:T(8,128)(2,1)S(1)}, u32[]{:S(2)}, u32[]{:S(2)}) async-start(bf16[4,128,1024]{2,1,0:T(8,128)(2,1)} %bitcast.1), calls=%async_computation | async-start | bytes 2097152 | tf_op jit(solution)/shard_map/all_to_all | solution.py:103
  19.0 5.7 %collective-permute-start.2 = (bf16[128,1024]{1,0:T(8,128)(2,1)S(1)}, bf16[128,1024]{1,0:T(8,128)(2,1)S(1)}, u32[]{:S(2)}, u32[]{:S(2)}) collective-permute-start(bf16[128,1024]{1,0:T(8,128)(2,1)S(1)} %pad_maximum_fusion), channel_id=1, source_target_pairs={{0,112},{16,0},{32,16},{48,32},{64,48},{80,64},{96,80},{112,96},{1... | collective-permute-start | bytes 786440 | tf_op jit(solution)/shard_map/ppermute | solution.py:55
  24.6 5.7 %collective-permute-done.2 = bf16[128,1024]{1,0:T(8,128)(2,1)S(1)} collective-permute-done((bf16[128,1024]{1,0:T(8,128)(2,1)S(1)}, bf16[128,1024]{1,0:T(8,128)(2,1)S(1)}, u32[]{:S(2)}, u32[]{:S(2)}) %collective-permute-start.2) | collective-permute-done | bytes 262176 | tf_op jit(solution)/shard_map/ppermute | solution.py:55
  30.3 3.5 %collective-permute-done.3 = bf16[128,1024]{1,0:T(8,128)(2,1)S(1)} collective-permute-done((bf16[128,1024]{1,0:T(8,128)(2,1)S(1)}, bf16[128,1024]{1,0:T(8,128)(2,1)S(1)}, u32[]{:S(2)}, u32[]{:S(2)}) %collective-permute-start.3) | collective-permute-done | bytes 262176 | tf_op jit(solution)/shard_map/ppermute | solution.py:55
  34.5 2.8 %collective-permute-start.4 = (bf16[1024,512]{1,0:T(8,128)(2,1)}, bf16[1024,512]{1,0:T(8,128)(2,1)S(1)}, u32[]{:S(2)}, u32[]{:S(2)}) collective-permute-start(bf16[1024,512]{1,0:T(8,128)(2,1)} %param.4), channel_id=1, source_target_pairs={{1,0},{2,1},{3,2},{0,3},{5,4},{6,5},{7,6},{4,7},{9,8},{10,9},{11,1... | collective-permute-start | bytes 3145736 | tf_op jit(solution)/shard_map/ppermute | solution.py:16
  40.0 3.5 %collective-permute-start.7 = (bf16[128,1024]{1,0:T(8,128)(2,1)}, bf16[128,1024]{1,0:T(8,128)(2,1)}, u32[]{:S(2)}, u32[]{:S(2)}) collective-permute-start(bf16[128,1024]{1,0:T(8,128)(2,1)} %copy-done.2), channel_id=1, source_target_pairs={{0,112},{16,0},{32,16},{48,32},{64,48},{80,64},{96,80},{112,96},{1... | collective-permute-start | bytes 786440 | tf_op jit(solution)/shard_map/ppermute | solution.py:55
  43.5 5.7 %collective-permute-done.9 = bf16[128,1024]{1,0:T(8,128)(2,1)} collective-permute-done((bf16[128,1024]{1,0:T(8,128)(2,1)}, bf16[128,1024]{1,0:T(8,128)(2,1)}, u32[]{:S(2)}, u32[]{:S(2)}) %collective-permute-start.9) | collective-permute-done | bytes 262176 | tf_op jit(solution)/shard_map/ppermute | solution.py:55
  52.3 4.4 %collective-permute-done.10 = bf16[128,1024]{1,0:T(8,128)(2,1)S(1)} collective-permute-done((bf16[128,1024]{1,0:T(8,128)(2,1)}, bf16[128,1024]{1,0:T(8,128)(2,1)S(1)}, u32[]{:S(2)}, u32[]{:S(2)}) %collective-permute-start.10) | collective-permute-done | bytes 262176 | tf_op jit(solution)/shard_map/ppermute | solution.py:55
  56.8 2.9 %collective-permute-done.4 = bf16[1024,512]{1,0:T(8,128)(2,1)S(1)} collective-permute-done((bf16[1024,512]{1,0:T(8,128)(2,1)}, bf16[1024,512]{1,0:T(8,128)(2,1)S(1)}, u32[]{:S(2)}, u32[]{:S(2)}) %collective-permute-start.4) | collective-permute-done | bytes 1048608 | tf_op jit(solution)/shard_map/ppermute | solution.py:16
  59.7 3.1 %collective-permute-done.5 = bf16[1024,512]{1,0:T(8,128)(2,1)S(1)} collective-permute-done((bf16[1024,512]{1,0:T(8,128)(2,1)}, bf16[1024,512]{1,0:T(8,128)(2,1)S(1)}, u32[]{:S(2)}, u32[]{:S(2)}) %collective-permute-start.5) | collective-permute-done | bytes 1048608 | tf_op jit(solution)/shard_map/ppermute | solution.py:16
  65.5 3.2 %collective-permute-start.13 = (bf16[64,1024]{1,0:T(8,128)(2,1)S(1)}, bf16[64,1024]{1,0:T(8,128)(2,1)S(1)}, u32[]{:S(2)}, u32[]{:S(2)}) collective-permute-start(bf16[64,1024]{1,0:T(8,128)(2,1)S(1)} %slice.64), channel_id=1, source_target_pairs={{0,112},{16,0},{32,16},{48,32},{64,48},{80,64},{96,80},{112,96},{1... | collective-permute-start | bytes 393224 | tf_op jit(solution)/shard_map/ppermute | solution.py:55
  74.7 3.1 %collective-permute-done.12 = bf16[512,512]{1,0:T(8,128)(2,1)S(1)} collective-permute-done((bf16[512,512]{1,0:T(8,128)(2,1)S(1)}, bf16[512,512]{1,0:T(8,128)(2,1)S(1)}, u32[]{:S(2)}, u32[]{:S(2)}) %collective-permute-start.12) | collective-permute-done | bytes 524320 | tf_op jit(solution)/shard_map/ppermute | solution.py:16
  80.4 3.3 %collective-permute-start.15 = (bf16[1024,1024]{1,0:T(8,128)(2,1)S(1)}, bf16[1024,1024]{1,0:T(8,128)(2,1)S(1)}, u32[]{:S(2)}, u32[]{:S(2)}) collective-permute-start(bf16[1024,1024]{1,0:T(8,128)(2,1)S(1)} %fusion.24), channel_id=1, source_target_pairs={{0,8},{8,0},{1,9},{9,1},{2,10},{10,2},{3,11},{11,3},{4,12},{12,4},... | collective-permute-start | bytes 6291464 | tf_op jit(solution)/shard_map/ppermute | solution.py:20
  90.9 3.1 %collective-permute-start.17 = (bf16[128,1024]{1,0:T(8,128)(2,1)S(1)}, bf16[128,1024]{1,0:T(8,128)(2,1)S(1)}, u32[]{:S(2)}, u32[]{:S(2)}) collective-permute-start(bf16[128,1024]{1,0:T(8,128)(2,1)S(1)} %get-tuple-element.48), channel_id=1, source_target_pairs={{0,112},{16,0},{32,16},{48,32},{64,48},{80,64},{96,80},{112,96},{1... | collective-permute-start | bytes 786440 | tf_op jit(solution)/shard_map/ppermute | solution.py:55
  94.2 3.6 %collective-permute-start.19 = (bf16[64,1024]{1,0:T(8,128)(2,1)S(1)}, bf16[64,1024]{1,0:T(8,128)(2,1)S(1)}, u32[]{:S(2)}, u32[]{:S(2)}) collective-permute-start(bf16[64,1024]{1,0:T(8,128)(2,1)S(1)} %get-tuple-element.50), channel_id=1, source_target_pairs={{0,96},{16,112},{32,0},{48,16},{64,32},{80,48},{96,64},{112,80},{1... | collective-permute-start | bytes 393224 | tf_op jit(solution)/shard_map/ppermute | solution.py:55
  97.7 5.8 %fusion.19 = bf16[1024,1024]{1,0:T(8,128)(2,1)} fusion(bf16[1024,1024]{1,0:T(8,128)(2,1)S(1)} %collective-permute-done.20, bf16[1024,1024]{1,0:T(8,128)(2,1)S(1)} %constant_dynamic-update-slice_fusion.2, bf16[1024,512]{1,0:T(8,128)(2,1)S(1)} %get-tuple-element.55, bf16[1024,512]{1,0:T(8,128)(2,1)S(1)} %get-tuple-element.53, ...), kind=kOutput, calls=%fused_computation.20 | convolution fusion | flops 4321181696 | bytes 10485760 | tf_op jit(solution)/shard_map/dot_general | solution.py:48
  104.8 2.9 %collective-permute-start.24 = (bf16[128,1024]{1,0:T(8,128)(2,1)}, bf16[128,1024]{1,0:T(8,128)(2,1)}, u32[]{:S(2)}, u32[]{:S(2)}) collective-permute-start(bf16[128,1024]{1,0:T(8,128)(2,1)} %get-tuple-element.47), channel_id=1, source_target_pairs={{0,112},{16,0},{32,16},{48,32},{64,48},{80,64},{96,80},{112,96},{1... | collective-permute-start | bytes 786440 | tf_op jit(solution)/shard_map/ppermute | solution.py:55
  108.3 3.9 %all-to-all-start.1 = ((bf16[8,128,1024]{2,1,0:T(8,128)(2,1)}), bf16[8,128,1024]{2,1,0:T(8,128)(2,1)S(1)}, u32[]{:S(2)}, u32[]{:S(2)}) async-start(bf16[8,128,1024]{2,1,0:T(8,128)(2,1)} %bitcast.17), calls=%async_computation.1 | async-start | bytes 4194304 | tf_op jit(solution)/shard_map/all_to_all | solution.py:159
  117.9 8.8 %collective-permute-done.21 = bf16[128,1024]{1,0:T(8,128)(2,1)S(1)} collective-permute-done((bf16[128,1024]{1,0:T(8,128)(2,1)S(1)}, bf16[128,1024]{1,0:T(8,128)(2,1)S(1)}, u32[]{:S(2)}, u32[]{:S(2)}) %collective-permute-start.21) | collective-permute-done | bytes 262176 | tf_op jit(solution)/shard_map/ppermute | solution.py:55
  130.7 4.5 %collective-permute-start.25 = (bf16[128,512]{1,0:T(8,128)(2,1)S(1)}, bf16[128,512]{1,0:T(8,128)(2,1)S(1)}, u32[]{:S(2)}, u32[]{:S(2)}) collective-permute-start(bf16[128,512]{1,0:T(8,128)(2,1)S(1)} %get-tuple-element.56), channel_id=1, source_target_pairs={{0,0},{1,129},{2,10},{3,139},{8,1},{9,130},{10,11},{11,136},{128,2... | collective-permute-start | bytes 393224 | tf_op jit(solution)/shard_map/ppermute | solution.py:37
  135.2 3.1 %collective-permute-start.26 = (bf16[128,512]{1,0:T(8,128)(2,1)S(1)}, bf16[128,512]{1,0:T(8,128)(2,1)S(1)}, u32[]{:S(2)}, u32[]{:S(2)}) collective-permute-start(bf16[128,512]{1,0:T(8,128)(2,1)S(1)} %get-tuple-element.57), channel_id=1, source_target_pairs={{0,2},{1,131},{2,8},{3,137},{8,3},{9,128},{10,9},{11,138},{128,0},... | collective-permute-start | bytes 393224 | tf_op jit(solution)/shard_map/ppermute | solution.py:37
  139.7 3.3 %collective-permute-done.26 = bf16[128,512]{1,0:T(8,128)(2,1)S(1)} collective-permute-done((bf16[128,512]{1,0:T(8,128)(2,1)S(1)}, bf16[128,512]{1,0:T(8,128)(2,1)S(1)}, u32[]{:S(2)}, u32[]{:S(2)}) %collective-permute-start.26) | collective-permute-done | bytes 131104 | tf_op jit(solution)/shard_map/ppermute | solution.py:37
  (89 shorter events, 45.0 us)
Async XLA Ops:
  0.6 12.0 %collective-permute-start = (bf16[128,512]{1,0:T(8,128)(2,1)}, bf16[128,512]{1,0:T(8,128)(2,1)S(1)}, u32[]{:S(2)}, u32[]{:S(2)}) collective-permute-start(bf16[128,512]{1,0:T(8,128)(2,1)} %param.5), channel_id=1, source_target_pairs={{0,0},{129,1},{10,2},{139,3},{1,8},{130,9},{11,10},{136,11},{2,128... | collective-permute-start | bytes 393224 | tf_op jit(solution)/shard_map/ppermute | solution.py:41
  7.7 7.7 %collective-permute-start.1 = (bf16[128,512]{1,0:T(8,128)(2,1)}, bf16[128,512]{1,0:T(8,128)(2,1)S(1)}, u32[]{:S(2)}, u32[]{:S(2)}) collective-permute-start(bf16[128,512]{1,0:T(8,128)(2,1)} %param.5), channel_id=1, source_target_pairs={{2,0},{131,1},{8,2},{137,3},{3,8},{128,9},{9,10},{138,11},{0,128},... | collective-permute-start | bytes 393224 | tf_op jit(solution)/shard_map/ppermute | solution.py:41
  15.4 18.4 %all-to-all-start = ((bf16[4,128,1024]{2,1,0:T(8,128)(2,1)}), bf16[4,128,1024]{2,1,0:T(8,128)(2,1)S(1)}, u32[]{:S(2)}, u32[]{:S(2)}) async-start(bf16[4,128,1024]{2,1,0:T(8,128)(2,1)} %bitcast.1), calls=%async_computation | async-start | bytes 2097152 | tf_op jit(solution)/shard_map/all_to_all | solution.py:103
  19.0 11.3 %collective-permute-start.2 = (bf16[128,1024]{1,0:T(8,128)(2,1)S(1)}, bf16[128,1024]{1,0:T(8,128)(2,1)S(1)}, u32[]{:S(2)}, u32[]{:S(2)}) collective-permute-start(bf16[128,1024]{1,0:T(8,128)(2,1)S(1)} %pad_maximum_fusion), channel_id=1, source_target_pairs={{0,112},{16,0},{32,16},{48,32},{64,48},{80,64},{96,80},{112,96},{1... | collective-permute-start | bytes 786440 | tf_op jit(solution)/shard_map/ppermute | solution.py:55
  24.6 9.2 %collective-permute-start.3 = (bf16[128,1024]{1,0:T(8,128)(2,1)S(1)}, bf16[128,1024]{1,0:T(8,128)(2,1)S(1)}, u32[]{:S(2)}, u32[]{:S(2)}) collective-permute-start(bf16[128,1024]{1,0:T(8,128)(2,1)S(1)} %pad_maximum_fusion), channel_id=1, source_target_pairs={{0,16},{16,32},{32,48},{48,64},{64,80},{80,96},{96,112},{112,0},{1... | collective-permute-start | bytes 786440 | tf_op jit(solution)/shard_map/ppermute | solution.py:55
  34.5 25.1 %collective-permute-start.4 = (bf16[1024,512]{1,0:T(8,128)(2,1)}, bf16[1024,512]{1,0:T(8,128)(2,1)S(1)}, u32[]{:S(2)}, u32[]{:S(2)}) collective-permute-start(bf16[1024,512]{1,0:T(8,128)(2,1)} %param.4), channel_id=1, source_target_pairs={{1,0},{2,1},{3,2},{0,3},{5,4},{6,5},{7,6},{4,7},{9,8},{10,9},{11,1... | collective-permute-start | bytes 3145736 | tf_op jit(solution)/shard_map/ppermute | solution.py:16
  37.4 25.4 %collective-permute-start.5 = (bf16[1024,512]{1,0:T(8,128)(2,1)}, bf16[1024,512]{1,0:T(8,128)(2,1)S(1)}, u32[]{:S(2)}, u32[]{:S(2)}) collective-permute-start(bf16[1024,512]{1,0:T(8,128)(2,1)} %param.4), channel_id=1, source_target_pairs={{3,0},{0,1},{1,2},{2,3},{7,4},{4,5},{5,6},{6,7},{11,8},{8,9},{9,10... | collective-permute-start | bytes 3145736 | tf_op jit(solution)/shard_map/ppermute | solution.py:16
  37.4 25.5 %collective-permute-start.6 = (bf16[512,1024]{1,0:T(8,128)(2,1)S(1)}, bf16[512,1024]{1,0:T(8,128)(2,1)}, u32[]{:S(2)}, u32[]{:S(2)}) collective-permute-start(bf16[512,1024]{1,0:T(8,128)(2,1)S(1)} %bitcast.13), channel_id=1, source_target_pairs={{0,4},{4,0},{1,5},{5,1},{2,6},{6,2},{3,7},{7,3},{8,12},{12,8},{9,1... | collective-permute-start | bytes 3145736 | tf_op jit(solution)/shard_map/ppermute | solution.py:20
  40.0 9.3 %collective-permute-start.9 = (bf16[128,1024]{1,0:T(8,128)(2,1)}, bf16[128,1024]{1,0:T(8,128)(2,1)}, u32[]{:S(2)}, u32[]{:S(2)}) collective-permute-start(bf16[128,1024]{1,0:T(8,128)(2,1)} %copy-done.4), channel_id=1, source_target_pairs={{0,16},{16,32},{32,48},{48,64},{64,80},{80,96},{96,112},{112,0},{1... | collective-permute-start | bytes 786440 | tf_op jit(solution)/shard_map/ppermute | solution.py:55
  40.0 9.3 %collective-permute-start.7 = (bf16[128,1024]{1,0:T(8,128)(2,1)}, bf16[128,1024]{1,0:T(8,128)(2,1)}, u32[]{:S(2)}, u32[]{:S(2)}) collective-permute-start(bf16[128,1024]{1,0:T(8,128)(2,1)} %copy-done.2), channel_id=1, source_target_pairs={{0,112},{16,0},{32,16},{48,32},{64,48},{80,64},{96,80},{112,96},{1... | collective-permute-start | bytes 786440 | tf_op jit(solution)/shard_map/ppermute | solution.py:55
  62.9 11.8 %collective-permute-start.11 = (bf16[512,512]{1,0:T(8,128)(2,1)S(1)}, bf16[512,512]{1,0:T(8,128)(2,1)S(1)}, u32[]{:S(2)}, u32[]{:S(2)}) collective-permute-start(bf16[512,512]{1,0:T(8,128)(2,1)S(1)} %slice.62), channel_id=1, source_target_pairs={{1,0},{2,1},{3,2},{0,3},{5,4},{6,5},{7,6},{4,7},{9,8},{10,9},{11,1... | collective-permute-start | bytes 1572872 | tf_op jit(solution)/shard_map/ppermute | solution.py:16
  65.4 12.4 %collective-permute-start.12 = (bf16[512,512]{1,0:T(8,128)(2,1)S(1)}, bf16[512,512]{1,0:T(8,128)(2,1)S(1)}, u32[]{:S(2)}, u32[]{:S(2)}) collective-permute-start(bf16[512,512]{1,0:T(8,128)(2,1)S(1)} %slice.63), channel_id=1, source_target_pairs={{3,0},{0,1},{1,2},{2,3},{7,4},{4,5},{5,6},{6,7},{11,8},{8,9},{9,10... | collective-permute-start | bytes 1572872 | tf_op jit(solution)/shard_map/ppermute | solution.py:16
  85.9 11.9 %collective-permute-start.20 = (bf16[1024,1024]{1,0:T(8,128)(2,1)S(1)}, bf16[1024,1024]{1,0:T(8,128)(2,1)S(1)}, u32[]{:S(2)}, u32[]{:S(2)}) collective-permute-start(bf16[1024,1024]{1,0:T(8,128)(2,1)S(1)} %constant_dynamic-update-slice_fusion.2), channel_id=1, source_target_pairs={{0,8},{8,0},{1,9},{9,1},{2,10},{10,2},{3,11},{11,3},{4,12},{12,4},... | collective-permute-start | bytes 6291464 | tf_op jit(solution)/shard_map/ppermute | solution.py:20
  90.9 16.7 %collective-permute-start.16 = (bf16[128,1024]{1,0:T(8,128)(2,1)S(1)}, bf16[128,1024]{1,0:T(8,128)(2,1)S(1)}, u32[]{:S(2)}, u32[]{:S(2)}) collective-permute-start(bf16[128,1024]{1,0:T(8,128)(2,1)S(1)} %get-tuple-element.49), channel_id=1, source_target_pairs={{0,16},{16,32},{32,48},{48,64},{64,80},{80,96},{96,112},{112,0},{1... | collective-permute-start | bytes 786440 | tf_op jit(solution)/shard_map/ppermute | solution.py:55
  90.9 16.7 %collective-permute-start.17 = (bf16[128,1024]{1,0:T(8,128)(2,1)S(1)}, bf16[128,1024]{1,0:T(8,128)(2,1)S(1)}, u32[]{:S(2)}, u32[]{:S(2)}) collective-permute-start(bf16[128,1024]{1,0:T(8,128)(2,1)S(1)} %get-tuple-element.48), channel_id=1, source_target_pairs={{0,112},{16,0},{32,16},{48,32},{64,48},{80,64},{96,80},{112,96},{1... | collective-permute-start | bytes 786440 | tf_op jit(solution)/shard_map/ppermute | solution.py:55
  94.1 10.7 %collective-permute-start.18 = (bf16[64,1024]{1,0:T(8,128)(2,1)S(1)}, bf16[64,1024]{1,0:T(8,128)(2,1)S(1)}, u32[]{:S(2)}, u32[]{:S(2)}) collective-permute-start(bf16[64,1024]{1,0:T(8,128)(2,1)S(1)} %get-tuple-element.51), channel_id=1, source_target_pairs={{0,32},{16,48},{32,64},{48,80},{64,96},{80,112},{96,0},{112,16},{1... | collective-permute-start | bytes 393224 | tf_op jit(solution)/shard_map/ppermute | solution.py:55
  94.2 13.5 %collective-permute-start.19 = (bf16[64,1024]{1,0:T(8,128)(2,1)S(1)}, bf16[64,1024]{1,0:T(8,128)(2,1)S(1)}, u32[]{:S(2)}, u32[]{:S(2)}) collective-permute-start(bf16[64,1024]{1,0:T(8,128)(2,1)S(1)} %get-tuple-element.50), channel_id=1, source_target_pairs={{0,96},{16,112},{32,0},{48,16},{64,32},{80,48},{96,64},{112,80},{1... | collective-permute-start | bytes 393224 | tf_op jit(solution)/shard_map/ppermute | solution.py:55
  97.7 20.2 %collective-permute-start.23 = (bf16[128,1024]{1,0:T(8,128)(2,1)}, bf16[128,1024]{1,0:T(8,128)(2,1)S(1)}, u32[]{:S(2)}, u32[]{:S(2)}) collective-permute-start(bf16[128,1024]{1,0:T(8,128)(2,1)} %get-tuple-element.46), channel_id=1, source_target_pairs={{0,16},{16,32},{32,48},{48,64},{64,80},{80,96},{96,112},{112,0},{1... | collective-permute-start | bytes 786440 | tf_op jit(solution)/shard_map/ppermute | solution.py:55
  104.8 13.1 %collective-permute-start.24 = (bf16[128,1024]{1,0:T(8,128)(2,1)}, bf16[128,1024]{1,0:T(8,128)(2,1)}, u32[]{:S(2)}, u32[]{:S(2)}) collective-permute-start(bf16[128,1024]{1,0:T(8,128)(2,1)} %get-tuple-element.47), channel_id=1, source_target_pairs={{0,112},{16,0},{32,16},{48,32},{64,48},{80,64},{96,80},{112,96},{1... | collective-permute-start | bytes 786440 | tf_op jit(solution)/shard_map/ppermute | solution.py:55
  108.3 35.4 %all-to-all-start.1 = ((bf16[8,128,1024]{2,1,0:T(8,128)(2,1)}), bf16[8,128,1024]{2,1,0:T(8,128)(2,1)S(1)}, u32[]{:S(2)}, u32[]{:S(2)}) async-start(bf16[8,128,1024]{2,1,0:T(8,128)(2,1)} %bitcast.17), calls=%async_computation.1 | async-start | bytes 4194304 | tf_op jit(solution)/shard_map/all_to_all | solution.py:159
  113.2 13.5 %collective-permute-start.21 = (bf16[128,1024]{1,0:T(8,128)(2,1)S(1)}, bf16[128,1024]{1,0:T(8,128)(2,1)S(1)}, u32[]{:S(2)}, u32[]{:S(2)}) collective-permute-start(bf16[128,1024]{1,0:T(8,128)(2,1)S(1)} %pad_maximum_fusion.1), channel_id=1, source_target_pairs={{0,32},{16,48},{32,64},{48,80},{64,96},{80,112},{96,0},{112,16},{1... | collective-permute-start | bytes 786440 | tf_op jit(solution)/shard_map/ppermute | solution.py:55
  116.3 13.1 %collective-permute-start.22 = (bf16[128,1024]{1,0:T(8,128)(2,1)S(1)}, bf16[128,1024]{1,0:T(8,128)(2,1)S(1)}, u32[]{:S(2)}, u32[]{:S(2)}) collective-permute-start(bf16[128,1024]{1,0:T(8,128)(2,1)S(1)} %pad_maximum_fusion.2), channel_id=1, source_target_pairs={{0,96},{16,112},{32,0},{48,16},{64,32},{80,48},{96,64},{112,80},{1... | collective-permute-start | bytes 786440 | tf_op jit(solution)/shard_map/ppermute | solution.py:55
  130.7 9.0 %collective-permute-start.25 = (bf16[128,512]{1,0:T(8,128)(2,1)S(1)}, bf16[128,512]{1,0:T(8,128)(2,1)S(1)}, u32[]{:S(2)}, u32[]{:S(2)}) collective-permute-start(bf16[128,512]{1,0:T(8,128)(2,1)S(1)} %get-tuple-element.56), channel_id=1, source_target_pairs={{0,0},{1,129},{2,10},{3,139},{8,1},{9,130},{10,11},{11,136},{128,2... | collective-permute-start | bytes 393224 | tf_op jit(solution)/shard_map/ppermute | solution.py:37
  135.2 7.8 %collective-permute-start.26 = (bf16[128,512]{1,0:T(8,128)(2,1)S(1)}, bf16[128,512]{1,0:T(8,128)(2,1)S(1)}, u32[]{:S(2)}, u32[]{:S(2)}) collective-permute-start(bf16[128,512]{1,0:T(8,128)(2,1)S(1)} %get-tuple-element.57), channel_id=1, source_target_pairs={{0,2},{1,131},{2,8},{3,137},{8,3},{9,128},{10,9},{11,138},{128,0},... | collective-permute-start | bytes 393224 | tf_op jit(solution)/shard_map/ppermute | solution.py:37
  (13 other events, 72.0 us)
